TPU v7x, 256 devices: a whole 4x4x8 slice. The times are simulated.
256 devices in a mesh: row: 8 (over y, x_hi), col: 32 (over x_lo, z, core).
Axes of the slice: x: 4 (x_hi: 2, x_lo: 2; x = x_hi * 2 + x_lo), y: 4, z: 8, core: 2. Of those that a mesh axis runs over, the one named last changes fastest.
Arguments:
- queries: bfloat16 [64, 512, 512], P('row', 'col'), may hold values from -6 to 6
- keys: bfloat16 [64, 512, 512], P('row', 'col'), may hold values from -6 to 6
- values: bfloat16 [64, 512, 512], P('row', 'col'), may hold values from -6 to 6
- grad_out: bfloat16 [64, 512, 512], P('row', 'col'), may hold values from -6 to 6
- rel_bias: float32 [8, 17, 17], replicated, may hold values from -4 to 4
- occupied: int32 [8, 32], replicated, may hold values 0 or 1
Outputs:
- grad_queries: bfloat16 [64, 512, 512], P('row', 'col')
- grad_keys: bfloat16 [64, 512, 512], P('row', 'col')
- grad_values: bfloat16 [64, 512, 512], P('row', 'col')
- grad_bias: float32 [8, 17, 17], replicated
All inputs are finite; a program needn't handle non-finite values.
Results may differ from a plain program's by a relative error of at most 0.015.
Values may be sent and summed in bfloat16 or wider, within the bound.
No kernel may reach another device: no remote copies, remote signals or barrier semaphores. Data moves between devices by JAX's collectives and lax.ppermute only.
A program may use at most 64 MiB of HBM per device.

v0:
```python
import jax
import jax.numpy as jnp
from jax import lax
from jax.sharding import PartitionSpec as P


def from_behind(value, axis, steps):
    count = lax.axis_size(axis)
    first, last = (max(0, -steps), min(count, count - steps))
    return lax.ppermute(value, axis, [(source, source + steps) for source in range(first, last)])


def with_halo(block, sides, width):
    for axis, dim in sides:
        count = lax.axis_size(axis)
        forward = [(i, i + 1) for i in range(count - 1)]
        backward = [(target, source) for source, target in forward]
        low = lax.ppermute(
            lax.slice_in_dim(block, block.shape[dim] - width, None, axis=dim), axis, forward
        )
        high = lax.ppermute(lax.slice_in_dim(block, 0, width, axis=dim), axis, backward)
        block = jnp.concatenate([low, block, high], axis=dim)
    return block


def offset_table(first_count, second_count, direction, window_span):
    table_shape = (first_count, second_count, window_span)
    first_index = lax.broadcasted_iota(jnp.int32, table_shape, 0)
    second_index = lax.broadcasted_iota(jnp.int32, table_shape, 1)
    slot_index = lax.broadcasted_iota(jnp.int32, table_shape, 2)
    return (direction * (second_index - first_index) == slot_index).astype(jnp.float32)


def expand_part(table_rows, table_cols, bias_part):
    partial_bias = jnp.einsum(
        "cqe,de->cqd", table_cols, bias_part, preferred_element_type=jnp.float32
    ).astype(jnp.bfloat16)
    return jnp.einsum("rpd,cqd->rcpq", table_rows, partial_bias, preferred_element_type=jnp.float32)


def expand_bias(table_rows, table_cols, bias_head):
    rows_low = table_rows.astype(jnp.bfloat16)
    cols_low = table_cols.astype(jnp.bfloat16)
    bias_high = bias_head.astype(jnp.bfloat16)
    bias_rest = (bias_head - bias_high.astype(jnp.float32)).astype(jnp.bfloat16)
    full_bias = expand_part(rows_low, cols_low, bias_high) + expand_part(
        rows_low, cols_low, bias_rest
    )
    return full_bias.reshape(
        full_bias.shape[0] * full_bias.shape[1], full_bias.shape[2] * full_bias.shape[3]
    )


def bias_gradient(grad_grid, window_span):
    tile_rows, tile_cols, padded_rows, padded_cols = grad_grid.shape
    by_rows = jnp.transpose(grad_grid, (0, 2, 1, 3)).reshape(
        tile_rows * padded_rows, tile_cols, padded_cols
    )
    by_rows = jnp.pad(by_rows, ((0, tile_rows), (0, 0), (0, 0)))
    by_rows = by_rows.reshape(tile_rows, padded_rows + 1, tile_cols, padded_cols)[:, :window_span]
    row_summed = jnp.sum(by_rows, axis=0).reshape(window_span, tile_cols * padded_cols)
    row_summed = jnp.pad(row_summed, ((0, 0), (0, tile_cols)))
    skewed = row_summed.reshape(window_span, tile_cols, padded_cols + 1)[:, :, :window_span]
    return jnp.sum(skewed, axis=1)


def allowed_pairs(table_rows, table_cols, cell_filled):
    row_inside = jnp.sum(table_rows, axis=2)
    col_inside = jnp.sum(table_cols, axis=2)
    joint = (
        row_inside[:, None, :, None] * col_inside[None, :, None, :] * cell_filled[None, None, :, :]
    )
    return joint.reshape(joint.shape[0] * joint.shape[1], joint.shape[2] * joint.shape[3]) > 0.5


def pick_tiles(extent, radius):
    cell_shape = (extent + 2 * radius, 3)
    position = lax.broadcasted_iota(jnp.int32, cell_shape, 0)
    tile_index = lax.broadcasted_iota(jnp.int32, cell_shape, 1)
    tile_of_cell = (position >= radius).astype(jnp.int32) + (position >= radius + extent).astype(
        jnp.int32
    )
    return (tile_of_cell == tile_index).astype(jnp.float32)


def neighbour_cells(nearby, tile_rows, tile_cols, radius):
    pick_rows = pick_tiles(tile_rows, radius)
    pick_cols = pick_tiles(tile_cols, radius)
    inner_rows = jnp.dot(pick_rows, nearby, precision=lax.Precision.HIGHEST)
    return jnp.dot(inner_rows, pick_cols.T, precision=lax.Precision.HIGHEST)


def head_slice(matrix, head_index, head_width):
    return lax.dynamic_slice_in_dim(matrix, head_index * head_width, head_width, 1)


def fold_columns(partials, radius):
    interior = partials.shape[2] - 2 * radius
    from_after = from_behind(partials[:, :, :radius].astype(jnp.bfloat16), "col", -1).astype(
        jnp.float32
    )
    from_before = from_behind(
        partials[:, :, radius + interior :].astype(jnp.bfloat16), "col", 1
    ).astype(jnp.float32)
    middle = partials[:, :, radius : radius + interior]
    middle = middle.at[:, :, :radius].add(from_before)
    return middle.at[:, :, interior - radius :].add(from_after)


def fold_rows(partials, radius):
    interior = partials.shape[1] - 2 * radius
    from_after = from_behind(partials[:, :radius].astype(jnp.bfloat16), "row", -1).astype(
        jnp.float32
    )
    from_before = from_behind(
        partials[:, radius + interior :].astype(jnp.bfloat16), "row", 1
    ).astype(jnp.float32)
    middle = partials[:, radius : radius + interior]
    middle = middle.at[:, :radius].add(from_before)
    return middle.at[:, interior - radius :].add(from_after)


def transposed_dot(left_matrix, right_matrix):
    return lax.dot_general(
        left_matrix, right_matrix, (((0,), (0,)), ((), ())), preferred_element_type=jnp.float32
    )


def rows_dot(left_matrix, right_matrix):
    return lax.dot_general(
        left_matrix, right_matrix, (((1,), (1,)), ((), ())), preferred_element_type=jnp.float32
    )


def shards(queries, keys, values, grad_out, rel_bias, occupied):
    tile_rows, tile_cols, model_width = queries.shape
    head_count = rel_bias.shape[0]
    window_span = rel_bias.shape[1]
    radius = (window_span - 1) // 2
    head_width = model_width // head_count
    score_scale = head_width ** (-0.5)
    padded_rows = tile_rows + 2 * radius
    padded_cols = tile_cols + 2 * radius
    query_count = tile_rows * tile_cols
    padded_count = padded_rows * padded_cols
    row_index = lax.axis_index("row")
    col_index = lax.axis_index("col")
    nearby = lax.dynamic_slice(jnp.pad(occupied, 1), (row_index, col_index), (3, 3)).astype(
        jnp.float32
    )
    own_tile = nearby[1, 1]
    cell_filled = neighbour_cells(nearby, tile_rows, tile_cols, radius)
    key_value_halo = with_halo(jnp.stack((keys, values)), (("row", 1), ("col", 2)), radius)
    key_matrix = key_value_halo[0].reshape(padded_count, model_width)
    value_matrix = key_value_halo[1].reshape(padded_count, model_width)
    query_matrix = queries.reshape(query_count, model_width)
    grad_matrix = grad_out.reshape(query_count, model_width)
    forward_rows = offset_table(tile_rows, padded_rows, 1, window_span)
    forward_cols = offset_table(tile_cols, padded_cols, 1, window_span)
    forward_allowed = allowed_pairs(forward_rows, forward_cols, cell_filled)
    partial_shape = (padded_count, model_width)

    def query_pass(head_index, carried):
        grad_query, grad_key, grad_value, log_total, delta_all, grad_bias = carried
        query_head = head_slice(query_matrix, head_index, head_width)
        key_head = head_slice(key_matrix, head_index, head_width)
        value_head = head_slice(value_matrix, head_index, head_width)
        grad_head = head_slice(grad_matrix, head_index, head_width)
        bias_head = lax.dynamic_index_in_dim(rel_bias, head_index, 0, keepdims=False)
        scores = rows_dot(query_head, key_head) * score_scale + expand_bias(
            forward_rows, forward_cols, bias_head
        )
        scores = jnp.where(forward_allowed, scores, -jnp.inf)
        row_max = jnp.max(scores, axis=1, keepdims=True)
        exponent = jnp.exp(scores - row_max)
        row_total = jnp.sum(exponent, axis=1, keepdims=True)
        weights = exponent / row_total
        grad_weights = rows_dot(grad_head, value_head)
        row_delta = jnp.sum(weights * grad_weights, axis=1, keepdims=True)
        grad_scores = weights * (grad_weights - row_delta)
        weights_low = weights.astype(jnp.bfloat16)
        grad_scores_low = grad_scores.astype(jnp.bfloat16)
        query_term = (
            jnp.dot(grad_scores_low, key_head, preferred_element_type=jnp.float32) * score_scale
        )
        grad_query = lax.dynamic_update_slice_in_dim(
            grad_query, query_term, head_index * head_width, 1
        )
        bias_term = bias_gradient(
            grad_scores.reshape(tile_rows, tile_cols, padded_rows, padded_cols), window_span
        )
        grad_bias = lax.dynamic_update_index_in_dim(grad_bias, bias_term, head_index, 0)
        log_total = lax.dynamic_update_slice_in_dim(
            log_total, row_max + jnp.log(row_total), head_index, 1
        )
        delta_all = lax.dynamic_update_slice_in_dim(delta_all, row_delta, head_index, 1)
        key_term = transposed_dot(grad_scores_low, query_head) * score_scale
        value_term = transposed_dot(weights_low, grad_head)
        grad_key = lax.dynamic_update_slice_in_dim(grad_key, key_term, head_index * head_width, 1)
        grad_value = lax.dynamic_update_slice_in_dim(
            grad_value, value_term, head_index * head_width, 1
        )
        return (grad_query, grad_key, grad_value, log_total, delta_all, grad_bias)

    initial = (
        jnp.zeros((query_count, model_width), jnp.float32),
        jnp.zeros(partial_shape, jnp.float32),
        jnp.zeros(partial_shape, jnp.float32),
        jnp.zeros((query_count, head_count), jnp.float32),
        jnp.zeros((query_count, head_count), jnp.float32),
        jnp.zeros((head_count, window_span, window_span), jnp.float32),
    )

    def run_queries():
        return lax.fori_loop(0, head_count, query_pass, initial)

    def skip_queries():
        return initial

    grad_query, grad_key, grad_value, log_total, delta_all, grad_bias = lax.cond(
        own_tile > 0.5, run_queries, skip_queries
    )
    bias_summed = lax.psum(grad_bias, ("row", "col"))
    query_grads = grad_query.astype(jnp.bfloat16).reshape(tile_rows, tile_cols, model_width)
    partials = jnp.stack((grad_key, grad_value)).reshape(2, padded_rows, padded_cols, model_width)
    owned_grads = fold_rows(fold_columns(partials, radius), radius)
    return (
        query_grads,
        owned_grads[0].astype(jnp.bfloat16),
        owned_grads[1].astype(jnp.bfloat16),
        bias_summed,
    )


def solution(mesh):
    placed = (
        P("row", "col", None),
        P("row", "col", None),
        P("row", "col", None),
        P("row", "col", None),
        P(),
        P(),
    )
    return jax.shard_map(
        shards,
        mesh=mesh,
        in_specs=placed,
        out_specs=(P("row", "col", None), P("row", "col", None), P("row", "col", None), P()),
        check_vma=False,
    )
```

profile of v0, /device:TPU:1, one launch (start us, length us, event | category | flops | bytes accessed | tf_op | source)
XLA Modules:
  0.0 288.9 jit_solution(15727028662749946175)
XLA Ops:
  2.9 6.1 %collective-permute-start = (bf16[2,8,16,512]{3,2,1,0:T(8,128)(2,1)S(1)}, bf16[2,8,16,512]{3,2,1,0:T(8,128)(2,1)S(1)}, u32[]{:S(2)}, u32[]{:S(2)}) collective-permute-start(bf16[2,8,16,512]{3,2,1,0:T(8,128)(2,1)S(1)} %pad_maximum_fusion.2), channel_id=1, source_target_pairs={{0,32},{32,64},{64,96},{96,128},{128,160},{160,192},{192,224},{1,3... | collective-permute-start | bytes 786440 | tf_op jit(solution)/shard_map/ppermute | solution.py:18
  13.5 6.8 %collective-permute-start.2 = (bf16[2,24,8,512]{3,2,1,0:T(8,128)(2,1)S(1)}, bf16[2,24,8,512]{3,2,1,0:T(8,128)(2,1)S(1)}, u32[]{:S(2)}, u32[]{:S(2)}) collective-permute-start(bf16[2,24,8,512]{3,2,1,0:T(8,128)(2,1)S(1)} %get-tuple-element.626), channel_id=1, source_target_pairs={{0,1},{1,2},{2,3},{3,4},{4,5},{5,6},{6,7},{7,8},{8,9},{9,10},{10,1... | collective-permute-start | bytes 1179656 | tf_op jit(solution)/shard_map/ppermute | solution.py:18
  20.3 1.9 collective-permute-start.3
  25.0 4.4 %collective-permute-done.3 = bf16[2,24,8,512]{3,2,1,0:T(8,128)(2,1)S(1)} collective-permute-done((bf16[2,24,8,512]{3,2,1,0:T(8,128)(2,1)S(1)}, bf16[2,24,8,512]{3,2,1,0:T(8,128)(2,1)S(1)}, u32[]{:S(2)}, u32[]{:S(2)}) %collective-permute-start.3) | collective-permute-done | bytes 393248 | tf_op jit(solution)/shard_map/ppermute | solution.py:21
  29.6 149.7 %conditional.1 = (f32[8,17,17]{2,1,0:T(8,128)S(1)}, bf16[8,16,512]{2,1,0:T(8,128)(2,1)S(1)}, f32[1,24,32,512]{3,2,1,0:T(8,128)}, f32[1,24,32,512]{3,2,1,0:T(8,128)}) conditional(s32[]{:T(128)} %bitcast.7, () %tuple.69, (bf16[8,16,512]{2,1,0:T(8,128)(2,1)}, bf16[2,24,32,512]{3,2,1,0:T(8,128)(2,1)S(1)}, bf16[8,16,512]{2,1,0:T(8,128)(2,1)}, ...), branch_computations={%region_0.1_spmd, %region_1.11_spmd} | conditional | flops 72604152 | bytes 37085184 | solution.py:220
  35.3 138.2 %while.32 = (s32[]{:T(128)}, bf16[128,512]{0,1:T(8,128)(2,1)}, f32[768,512]{0,1:T(8,128)}, f32[768,512]{0,1:T(8,128)}, f32[8,17,17]{2,1,0:T(8,128)}, /*index=5*/...) while((s32[]{:T(128)}, bf16[128,512]{0,1:T(8,128)(2,1)}, ...), condition=%wide.region_10.10_spmd.clone, body=%wide.region_4.9_spmd.clone.sunk | while | flops 72592888 | bytes 17553728 | solution.py:215
  42.7 1.7 convolution_dynamic-update-slice_fusion.2
  47.7 2.0 copy.96
  61.6 1.7 fusion.97
  65.0 2.0 copy.96
  77.2 1.7 convolution_dynamic-update-slice_fusion.2
  78.9 1.7 fusion.97
  82.3 2.0 copy.96
  94.5 1.7 convolution_dynamic-update-slice_fusion.2
  99.6 2.0 copy.96
  111.8 1.7 convolution_dynamic-update-slice_fusion.2
  113.5 1.7 fusion.97
  116.8 2.0 copy.96
  130.8 1.7 fusion.97
  134.1 2.0 copy.96
  146.3 1.7 convolution_dynamic-update-slice_fusion.2
  151.4 2.0 copy.96
  163.6 1.7 convolution_dynamic-update-slice_fusion.2
  165.3 1.7 fusion.97
  168.7 2.0 copy.96
  174.6 3.1 %copy.54 = f32[768,512]{1,0:T(8,128)} copy(f32[768,512]{0,1:T(8,128)} %get-tuple-element.464) | data formatting | bytes 3145728 | tf_op jit(solution)/shard_map/cond/branch_1_fun/while | solution.py:215
  182.8 1.9 collective-permute-start.4
  184.7 2.4 collective-permute-start.5
  187.3 2.1 collective-permute-done.4
  189.5 4.3 %collective-permute-done.5 = bf16[2,24,8,512]{3,2,1,0:T(8,128)(2,1)S(1)} collective-permute-done((bf16[2,24,8,512]{3,2,1,0:T(8,128)(2,1)S(1)}, bf16[2,24,8,512]{3,2,1,0:T(8,128)(2,1)S(1)}, u32[]{:S(2)}, u32[]{:S(2)}) %collective-permute-start.5) | collective-permute-done | bytes 393248 | tf_op jit(solution)/shard_map/ppermute | solution.py:10
  194.2 5.9 %collective-permute-start.6 = (bf16[2,8,16,512]{3,2,1,0:T(8,128)(2,1)S(1)}, bf16[2,8,16,512]{3,2,1,0:T(8,128)(2,1)S(1)}, u32[]{:S(2)}, u32[]{:S(2)}) collective-permute-start(bf16[2,8,16,512]{3,2,1,0:T(8,128)(2,1)S(1)} %get-tuple-element.624), channel_id=1, source_target_pairs={{0,32},{32,64},{64,96},{96,128},{128,160},{160,192},{192,224},{1,3... | collective-permute-start | bytes 786440 | tf_op jit(solution)/shard_map/ppermute | solution.py:10
  201.4 86.7 %psum.7 = f32[8,17,17]{2,0,1:T(8,128)} all-reduce(f32[8,17,17]{2,0,1:T(8,128)S(1)} %copy.61), channel_id=1, replica_groups=mesh['row'=8,'col'=32] {'row','col'}, use_global_device_ids=true, to_apply=%region_11.12 | all-reduce | flops 2312 | bytes 18496 | tf_op jit(solution)/shard_map/psum | solution.py:223
  (254 shorter events, 125.8 us)
Async XLA Ops:
  1.6 9.2 %collective-permute-start.1 = (bf16[2,8,16,512]{3,2,1,0:T(8,128)(2,1)S(1)}, bf16[2,8,16,512]{3,2,1,0:T(8,128)(2,1)S(1)}, u32[]{:S(2)}, u32[]{:S(2)}) collective-permute-start(bf16[2,8,16,512]{3,2,1,0:T(8,128)(2,1)S(1)} %pad_maximum_fusion.2), channel_id=1, source_target_pairs={{32,0},{64,32},{96,64},{128,96},{160,128},{192,160},{224,192},{33,... | collective-permute-start | bytes 786440 | tf_op jit(solution)/shard_map/ppermute | solution.py:21
  2.9 9.4 %collective-permute-start = (bf16[2,8,16,512]{3,2,1,0:T(8,128)(2,1)S(1)}, bf16[2,8,16,512]{3,2,1,0:T(8,128)(2,1)S(1)}, u32[]{:S(2)}, u32[]{:S(2)}) collective-permute-start(bf16[2,8,16,512]{3,2,1,0:T(8,128)(2,1)S(1)} %pad_maximum_fusion.2), channel_id=1, source_target_pairs={{0,32},{32,64},{64,96},{96,128},{128,160},{160,192},{192,224},{1,3... | collective-permute-start | bytes 786440 | tf_op jit(solution)/shard_map/ppermute | solution.py:18
  10.1 19.4 %copy-start.3 = (bf16[8,16,512]{2,1,0:T(8,128)(2,1)S(1)}, bf16[8,16,512]{2,1,0:T(8,128)(2,1)}, u32[]{:S(2)}) copy-start(bf16[8,16,512]{2,1,0:T(8,128)(2,1)} %param.24) | copy-start | bytes 393220
  10.1 19.4 %copy-start.4 = (bf16[8,16,512]{2,1,0:T(8,128)(2,1)S(1)}, bf16[8,16,512]{2,1,0:T(8,128)(2,1)}, u32[]{:S(2)}) copy-start(bf16[8,16,512]{2,1,0:T(8,128)(2,1)} %param.23) | copy-start | bytes 393220
  13.5 11.6 %collective-permute-start.2 = (bf16[2,24,8,512]{3,2,1,0:T(8,128)(2,1)S(1)}, bf16[2,24,8,512]{3,2,1,0:T(8,128)(2,1)S(1)}, u32[]{:S(2)}, u32[]{:S(2)}) collective-permute-start(bf16[2,24,8,512]{3,2,1,0:T(8,128)(2,1)S(1)} %get-tuple-element.626), channel_id=1, source_target_pairs={{0,1},{1,2},{2,3},{3,4},{4,5},{5,6},{6,7},{7,8},{8,9},{9,10},{10,1... | collective-permute-start | bytes 1179656 | tf_op jit(solution)/shard_map/ppermute | solution.py:18
  20.3 9.1 %collective-permute-start.3 = (bf16[2,24,8,512]{3,2,1,0:T(8,128)(2,1)S(1)}, bf16[2,24,8,512]{3,2,1,0:T(8,128)(2,1)S(1)}, u32[]{:S(2)}, u32[]{:S(2)}) collective-permute-start(bf16[2,24,8,512]{3,2,1,0:T(8,128)(2,1)S(1)} %get-tuple-element.627), channel_id=1, source_target_pairs={{1,0},{2,1},{3,2},{4,3},{5,4},{6,5},{7,6},{8,7},{9,8},{10,9},{11,1... | collective-permute-start | bytes 1179656 | tf_op jit(solution)/shard_map/ppermute | solution.py:21
  32.8 2.5 copy-start.2
  37.7 1.1 copy-start
  54.9 1.1 copy-start
  72.2 1.1 copy-start
  89.5 1.1 copy-start
  106.8 1.1 copy-start
  124.1 1.1 copy-start
  141.3 1.1 copy-start
  158.6 1.1 copy-start
  174.5 3.2 %copy-start.1 = (f32[768,512]{0,1:T(8,128)S(1)}, f32[768,512]{0,1:T(8,128)}, u32[]{:S(2)}) copy-start(f32[768,512]{0,1:T(8,128)} %get-tuple-element.465) | copy-start | bytes 4718596 | tf_op jit(solution)/shard_map/cond
  177.7 1.6 copy-start.5
  179.3 1.6 copy-start.6
  182.8 6.6 %collective-permute-start.4 = (bf16[2,24,8,512]{3,2,1,0:T(8,128)(2,1)S(1)}, bf16[2,24,8,512]{3,2,1,0:T(8,128)(2,1)S(1)}, u32[]{:S(2)}, u32[]{:S(2)}) collective-permute-start(bf16[2,24,8,512]{3,2,1,0:T(8,128)(2,1)S(1)} %get-tuple-element.623), channel_id=1, source_target_pairs={{0,1},{1,2},{2,3},{3,4},{4,5},{5,6},{6,7},{7,8},{8,9},{9,10},{10,1... | collective-permute-start | bytes 1179656 | tf_op jit(solution)/shard_map/ppermute | solution.py:10
  184.7 9.1 %collective-permute-start.5 = (bf16[2,24,8,512]{3,2,1,0:T(8,128)(2,1)S(1)}, bf16[2,24,8,512]{3,2,1,0:T(8,128)(2,1)S(1)}, u32[]{:S(2)}, u32[]{:S(2)}) collective-permute-start(bf16[2,24,8,512]{3,2,1,0:T(8,128)(2,1)S(1)} %get-tuple-element.622), channel_id=1, source_target_pairs={{1,0},{2,1},{3,2},{4,3},{5,4},{6,5},{7,6},{8,7},{9,8},{10,9},{11,1... | collective-permute-start | bytes 1179656 | tf_op jit(solution)/shard_map/ppermute | solution.py:10
  194.2 93.9 %collective-permute-start.6 = (bf16[2,8,16,512]{3,2,1,0:T(8,128)(2,1)S(1)}, bf16[2,8,16,512]{3,2,1,0:T(8,128)(2,1)S(1)}, u32[]{:S(2)}, u32[]{:S(2)}) collective-permute-start(bf16[2,8,16,512]{3,2,1,0:T(8,128)(2,1)S(1)} %get-tuple-element.624), channel_id=1, source_target_pairs={{0,32},{32,64},{64,96},{96,128},{128,160},{160,192},{192,224},{1,3... | collective-permute-start | bytes 786440 | tf_op jit(solution)/shard_map/ppermute | solution.py:10
  200.1 88.0 %collective-permute-start.7 = (bf16[2,8,16,512]{3,2,1,0:T(8,128)(2,1)S(1)}, bf16[2,8,16,512]{3,2,1,0:T(8,128)(2,1)S(1)}, u32[]{:S(2)}, u32[]{:S(2)}) collective-permute-start(bf16[2,8,16,512]{3,2,1,0:T(8,128)(2,1)S(1)} %get-tuple-element.625), channel_id=1, source_target_pairs={{32,0},{64,32},{96,64},{128,96},{160,128},{192,160},{224,192},{33,... | collective-permute-start | bytes 786440 | tf_op jit(solution)/shard_map/ppermute | solution.py:10
where the time goes:
time: 292 us; the launch traced here: 289 us
  blocking collectives  86.7 us (30%)
  local copies, waits for them, and re-layouts  81.1 us (28%)
  matrix products  62.8 us (22%)
  starting transfers between devices  27.7 us (9%)
  waiting for transfers between devices  14.4 us (5%)
  other arithmetic  13.7 us (5%)
    psum x1, blocking collectives, shards(): bias_summed = lax.psum(grad_bias, ('row', 'col'))  86.7 us
    reshape x16, local copies, waits for them, and re-layouts, query_pass(): grad_scores.reshape(tile_rows, tile_cols, padded_rows, padded_cols)  28.7 us
    dot_general x16, matrix products, transposed_dot(): lax.dot_general(left_matrix, right_matrix, (((0,), (0,)), ((), ())), pref...  27.6 us
    dot_general x16, matrix products, rows_dot(): lax.dot_general(left_matrix, right_matrix, (((1,), (1,)), ((), ())), pref...  19.8 us
    ppermute x2, starting transfers between devices, with_halo(): lax.ppermute(lax.slice_in_dim(block, block.shape[dim] - width, None, axis...  13 us
    ppermute x4, starting transfers between devices, from_behind(): lax.ppermute(value, axis, [(source, source + steps) for source in range(f...  11.6 us
    dot_general x8, matrix products, query_pass(): jnp.dot(grad_scores_low, key_head, preferred_element_type=jnp.float32)  7.59 us
    dot_general x16, matrix products, expand_part(): jnp.einsum('rpd,cqd->rcpq', table_rows, partial_bias, preferred_element_t...  7.44 us
  transfers between devices with their start and end apart: 8, of which 6 were waited for; matrix products, arithmetic and copies ran while one was open for 1% of the time, Pallas kernels for 0%

commit v1 on v0

v1 whole, which is shorter than its diff:
```python
import functools

import jax
import jax.numpy as jnp
from jax import lax
from jax.experimental import pallas as pl
from jax.experimental.pallas import tpu as pltpu
from jax.sharding import PartitionSpec as P

LOG2E = 1.4426950408889634
MASKED = -1e30
VMEM_SPEC = pl.BlockSpec(memory_space=pltpu.VMEM)
SMEM_SPEC = pl.BlockSpec(memory_space=pltpu.SMEM)


def lanes_of(shape):
    return lax.broadcasted_iota(jnp.int32, shape, len(shape) - 1)


def swap_halves(array):
    return pltpu.roll(array, 64, 1)


def pack_kernel(q_ref, k_ref, v_ref, g_ref, out_ref):
    low = lanes_of((128, 128)) < 64
    for pair in range(4):
        lanes = pl.ds(128 * pair, 128)

        def load(ref):
            return ref[:, :, lanes].astype(jnp.float32)

        def by_halves(block):
            split = block.reshape(8, 2, 8, 128)
            return jnp.concatenate(
                [split[:, half].reshape(64, 128) for half in range(2)], axis=0
            )

        query = load(q_ref).reshape(128, 128) * 0.125
        grad = load(g_ref).reshape(128, 128)
        key = by_halves(load(k_ref))
        value = by_halves(load(v_ref))
        for at, first, second in ((0, query, grad), (128, key, value)):
            even = jnp.where(low, first, swap_halves(second))
            odd = jnp.where(low, swap_halves(first), second)
            out_ref[2 * pair, at : at + 128, :] = even.astype(jnp.bfloat16)
            out_ref[2 * pair + 1, at : at + 128, :] = odd.astype(jnp.bfloat16)


def pack(queries, keys, values, grad_out):
    return pl.pallas_call(
        pack_kernel,
        out_shape=jax.ShapeDtypeStruct((8, 256, 128), jnp.bfloat16),
        in_specs=[VMEM_SPEC] * 4,
        out_specs=VMEM_SPEC,
        name="pack",
    )(queries, keys, values, grad_out)


def build_table(head, bias_ref, rows_ref, table_ref):
    lane = lanes_of((544, 128))
    sub = lax.broadcasted_iota(jnp.int32, (544, 128), 0)
    rows_ref[...] = jnp.zeros_like(rows_ref)
    for a in range(17):
        rows_ref[a : a + 1, 0:17] = bias_ref[a, pl.ds(head, 1), :]
    spread = jnp.concatenate(
        [jnp.broadcast_to(rows_ref[a : a + 1, :], (32, 128)) for a in range(17)], axis=0
    )
    b_index = sub & 31
    column = jnp.sum(jnp.where(lane == b_index, spread, 0.0), axis=1, keepdims=True)
    skewed = jnp.where(b_index < 17, column * LOG2E, MASKED)
    query_col = lane & 15
    for bit in (1, 2, 4, 8):
        skewed = jnp.where((query_col & bit) > 0, pltpu.roll(skewed, bit, 0), skewed)
    blocks = skewed.reshape(17, 32, 128)
    empty = jnp.full((7, 32, 128), MASKED, jnp.float32)
    padded = jnp.concatenate([empty, blocks, empty], axis=0)
    query_row = lanes_of((24, 32, 128)) >> 4
    table = padded[7:31]
    for row in range(1, 8):
        table = jnp.where(query_row == row, padded[7 - row : 31 - row], table)
    table = table.reshape(3, 8, 4, 8, 128)
    for chunk in range(4):
        table_ref[:, chunk] = table[:, :, chunk]


def contract_bias(sums_ref, skew_ref, bias_out_ref):
    query_row = lanes_of((17, 8, 128)) >> 4
    for chunk in range(4):
        by_row = sums_ref[:, chunk].reshape(24, 8, 128)
        picked = by_row[0:17]
        for row in range(1, 8):
            picked = jnp.where(query_row == row, by_row[row : row + 17], picked)
        skew_ref[:, chunk] = picked
    skewed = skew_ref[...].reshape(544, 128)
    query_col = lanes_of((544, 128)) & 15
    for bit in (1, 2, 4, 8):
        skewed = jnp.where((query_col & bit) > 0, pltpu.roll(skewed, 544 - bit, 0), skewed)
    skewed = jnp.concatenate([skewed, jnp.zeros((96, 128), jnp.float32)], axis=0)
    total = lax.dot_general(
        jnp.ones((8, 128), jnp.float32),
        skewed,
        (((1,), (1,)), ((), ())),
        precision=lax.Precision.HIGHEST,
        preferred_element_type=jnp.float32,
    )
    rows = [total[0:1, 128 * k : 128 * k + 128] for k in range(5)]
    rows.append(jnp.zeros((3, 128), jnp.float32))
    block = jnp.concatenate(rows, axis=0)
    bias_out_ref[...] = jnp.broadcast_to(block[None], bias_out_ref.shape)


def main_kernel(
    occ_ref,
    bias_ref,
    x_ref,
    left_ref,
    right_ref,
    dq_ref,
    own_ref,
    out_left_ref,
    out_right_ref,
    bias_out_ref,
    rows_ref,
    table_ref,
    sums_ref,
    skew_ref,
    kv_ref,
    kt_ref,
    qg_ref,
    p_ref,
):
    head = lax.axis_index("row")
    col = lax.axis_index("col")
    col_count = occ_ref.shape[1]
    build_table(head, bias_ref, rows_ref, table_ref)
    sums_ref[...] = jnp.zeros_like(sums_ref)
    for edge in (0, 9):
        kv_ref[edge] = jnp.zeros((256, 128), jnp.bfloat16)
        kt_ref[edge] = jnp.zeros((128, 256), jnp.bfloat16)
        qg_ref[edge] = jnp.zeros((256, 128), jnp.bfloat16)
    p_ref[1, :, 0:256] = jnp.zeros((256, 256), jnp.bfloat16)
    p_ref[8, :, 512:768] = jnp.zeros((256, 256), jnp.bfloat16)
    low = lanes_of((128, 128)) < 64

    def stage(j, carry):
        kv_ref[j + 1, 0:64] = left_ref[j]
        kv_ref[j + 1, 64:192] = x_ref[j, 128:256]
        kv_ref[j + 1, 192:256] = right_ref[j]
        kt_ref[j + 1] = jnp.transpose(kv_ref[j + 1].astype(jnp.float32)).astype(jnp.bfloat16)
        query_grad = x_ref[j, 0:128].astype(jnp.float32)
        qg_ref[j + 1, 0:128] = jnp.where(low, query_grad, 0.0).astype(jnp.bfloat16)
        qg_ref[j + 1, 128:256] = jnp.where(low, 0.0, query_grad).astype(jnp.bfloat16)
        return carry

    lax.fori_loop(0, 8, stage, 0)

    def filled(row, at):
        inside = (row >= 0) & (row < 8) & (at >= 0) & (at < col_count)
        value = occ_ref[jnp.clip(row, 0, 7), jnp.clip(at, 0, col_count - 1)]
        return inside & (value > 0)

    def penalty(row, at):
        return jnp.where(filled(row, at), jnp.float32(0.0), jnp.float32(MASKED))

    def tile(i, carry):
        keys = kv_ref[pl.ds(i, 3)].reshape(768, 128)
        both = lax.dot_general(
            keys, qg_ref[i + 1], (((1,), (1,)), ((), ())), preferred_element_type=jnp.float32
        )
        scores, grads = both[:, 0:128], both[:, 128:256]
        shifted = []
        for step in range(3):
            row = i - 1 + step
            own = penalty(row, col)
            marks = (penalty(row, col - 1), own, own, penalty(row, col + 1))
            for chunk in range(4):
                at = 256 * step + 64 * chunk
                bias = table_ref[step, chunk].reshape(64, 128)
                shifted.append(scores[at : at + 64] * LOG2E + (bias + marks[chunk]))
        shifted = jnp.concatenate(shifted, axis=0)
        top = jnp.max(shifted, axis=0, keepdims=True)
        exponent = jnp.exp2(shifted - top)
        total = jnp.sum(exponent, axis=0, keepdims=True)
        weighted = jnp.sum(exponent * grads, axis=0, keepdims=True)
        inverse = 1.0 / total
        delta = weighted * inverse
        used = jnp.where(filled(i, col), jnp.float32(1.0), jnp.float32(0.0))
        weights = exponent * (inverse * used)
        grad_scores = weights * (grads - delta)
        sums_ref[...] += grad_scores.reshape(3, 4, 8, 8, 128)
        weights_low = weights.astype(jnp.bfloat16)
        grad_low = grad_scores.astype(jnp.bfloat16)
        grad_query = jnp.zeros((128, 128), jnp.float32)
        for step in range(3):
            part = grad_low[256 * step : 256 * step + 256]
            slot = 256 * (2 - step)
            p_ref[i + step, :, slot : slot + 128] = part
            p_ref[i + step, :, slot + 128 : slot + 256] = weights_low[256 * step : 256 * step + 256]
            grad_query += jnp.dot(kt_ref[i + step], part, preferred_element_type=jnp.float32)
        grad_query = jnp.transpose(grad_query * 0.125)
        packed = jnp.where(low[0:64], grad_query[0:64], swap_halves(grad_query[64:128]))
        dq_ref[i] = packed.astype(jnp.bfloat16)
        return carry

    lax.fori_loop(0, 8, tile, 0)

    def keys_pass(j, carry):
        result = jnp.dot(
            p_ref[j + 1],
            qg_ref[pl.ds(j, 3)].reshape(768, 128),
            preferred_element_type=jnp.float32,
        )
        out_left_ref[j] = result[0:64].astype(jnp.bfloat16)
        own_ref[j] = result[64:192]
        out_right_ref[j] = result[192:256].astype(jnp.bfloat16)
        return carry

    lax.fori_loop(0, 8, keys_pass, 0)
    contract_bias(sums_ref, skew_ref, bias_out_ref)


def main(occupied, bias, blocks, left, right, col_count):
    halo = jax.ShapeDtypeStruct((8, 64, 128), jnp.bfloat16)
    return pl.pallas_call(
        main_kernel,
        out_shape=(
            halo,
            jax.ShapeDtypeStruct((8, 128, 128), jnp.float32),
            halo,
            halo,
            jax.ShapeDtypeStruct((col_count, 8, 128), jnp.float32),
        ),
        in_specs=[SMEM_SPEC] + [VMEM_SPEC] * 4,
        out_specs=(VMEM_SPEC,) * 5,
        scratch_shapes=[
            pltpu.VMEM((24, 128), jnp.float32),
            pltpu.VMEM((3, 4, 8, 8, 128), jnp.float32),
            pltpu.VMEM((3, 4, 8, 8, 128), jnp.float32),
            pltpu.VMEM((17, 4, 8, 128), jnp.float32),
            pltpu.VMEM((10, 256, 128), jnp.bfloat16),
            pltpu.VMEM((10, 128, 256), jnp.bfloat16),
            pltpu.VMEM((10, 256, 128), jnp.bfloat16),
            pltpu.VMEM((10, 256, 768), jnp.bfloat16),
        ],
        compiler_params=pltpu.CompilerParams(vmem_limit_bytes=40 << 20),
        name="attention_backward",
    )(occupied, bias, blocks, left, right)


def combine_kernel(dq_ref, own_ref, left_ref, right_ref, bias_ref, out_ref):
    total = jnp.sum(bias_ref[...], axis=0)
    high = total.astype(jnp.bfloat16).astype(jnp.float32)
    rest = total - high
    middle = rest.astype(jnp.bfloat16).astype(jnp.float32)
    pieces = jnp.concatenate([high, middle, rest - middle, jnp.zeros_like(total)], axis=0)
    pieces = pieces.astype(jnp.bfloat16)
    for i in range(8):
        out_ref[i, 0:64] = dq_ref[i]
        for at, ref in ((0, left_ref), (64, right_ref)):
            summed = own_ref[i, at : at + 64] + ref[i].astype(jnp.float32)
            out_ref[i, 64 + at : 128 + at] = summed.astype(jnp.bfloat16)
        out_ref[i, 192:224] = pieces


def combine(dq, own, left, right, bias):
    return pl.pallas_call(
        combine_kernel,
        out_shape=jax.ShapeDtypeStruct((8, 224, 128), jnp.bfloat16),
        in_specs=[VMEM_SPEC] * 5,
        out_specs=VMEM_SPEC,
        name="combine",
    )(dq, own, left, right, bias)


def unpack_kernel(z_ref, gq_ref, gk_ref, gv_ref, gb_ref, bias_ref):
    low = lanes_of((128, 128)) < 64

    def by_rows(block):
        split = block.reshape(2, 8, 8, 128)
        return jnp.concatenate([split[0], split[1]], axis=1)

    for pair in range(4):
        lanes = pl.ds(128 * pair, 128)
        even = z_ref[2 * pair].astype(jnp.float32)
        odd = z_ref[2 * pair + 1].astype(jnp.float32)
        first = jnp.where(low[0:64], even[0:64], swap_halves(odd[0:64]))
        second = jnp.where(low[0:64], swap_halves(even[0:64]), odd[0:64])
        query = jnp.concatenate([first, second], axis=0)
        gq_ref[:, :, lanes] = query.reshape(8, 16, 128).astype(jnp.bfloat16)
        key = jnp.where(low, even[64:192], swap_halves(odd[64:192]))
        value = jnp.where(low, swap_halves(even[64:192]), odd[64:192])
        gk_ref[:, :, lanes] = by_rows(key).astype(jnp.bfloat16)
        gv_ref[:, :, lanes] = by_rows(value).astype(jnp.bfloat16)
        for head, block in ((2 * pair, even), (2 * pair + 1, odd)):
            bias_ref[head] = block[192:200] + block[200:208] + block[208:216]
    for a in range(17):
        row = bias_ref[:, a // 4, :]
        if a % 4:
            row = pltpu.roll(row, 128 - 32 * (a % 4), 1)
        gb_ref[a] = row[:, 0:17]


def unpack(blocks):
    token = jax.ShapeDtypeStruct((8, 16, 512), jnp.bfloat16)
    return pl.pallas_call(
        unpack_kernel,
        out_shape=(token, token, token, jax.ShapeDtypeStruct((17, 8, 17), jnp.float32)),
        in_specs=[VMEM_SPEC],
        out_specs=(VMEM_SPEC,) * 4,
        scratch_shapes=[pltpu.VMEM((8, 8, 128), jnp.float32)],
        name="unpack",
    )(blocks)


def shards(queries, keys, values, grad_out, rel_bias, occupied):
    col_count = lax.axis_size("col")
    rightward = [(i, i + 1) for i in range(col_count - 1)]
    leftward = [(i + 1, i) for i in range(col_count - 1)]
    packed = pack(queries, keys, values, grad_out)
    blocks = lax.all_to_all(packed, "row", 0, 0)
    from_left = lax.ppermute(blocks[:, 192:256], "col", rightward)
    from_right = lax.ppermute(blocks[:, 128:192], "col", leftward)
    bias = jnp.transpose(rel_bias, (1, 0, 2))
    dq, own, out_left, out_right, bias_part = main(
        occupied, bias, blocks, from_left, from_right, col_count
    )
    share_left = lax.ppermute(out_right, "col", rightward)
    share_right = lax.ppermute(out_left, "col", leftward)
    bias_parts = lax.all_to_all(bias_part, "col", 0, 0)
    returned = lax.all_to_all(combine(dq, own, share_left, share_right, bias_parts), "row", 0, 0)
    grad_query, grad_key, grad_value, grad_bias = unpack(returned)
    return grad_query, grad_key, grad_value, jnp.transpose(grad_bias, (1, 0, 2))


def solution(mesh):
    token = P("row", "col", None)
    return jax.shard_map(
        shards,
        mesh=mesh,
        in_specs=(token, token, token, token, P(), P()),
        out_specs=(token, token, token, P()),
        check_vma=False,
    )
```

time: 292 us -> 85.1 us (0.29)
  local copies, waits for them, and re-layouts: 81.1 us -> 2.16 us
  matrix products: 62.8 us -> 0 us
  blocking collectives: 86.7 us -> 32.6 us
  Pallas kernels: 0 us -> 18.9 us
  other arithmetic: 13.7 us -> 0 us
  waiting for transfers between devices: 14.4 us -> 6.58 us
  starting transfers between devices: 27.7 us -> 23.6 us
    psum x1 -> x0, blocking collectives: 86.7 us -> none  [shards(): bias_summed = lax.psum(grad_bias, ('row', 'col'))]
    dot_general x58 -> x0, matrix products: 62.8 us -> none  [the longest x16 27.6 us: transposed_dot(): lax.dot_general(left_matrix, right_matrix, (((0,), (0,)), ((), ())), pref...]
    reshape x56 -> x0, local copies, waits for them, and re-layouts: 44.1 us -> none  [the longest x16 28.7 us: query_pass(): grad_scores.reshape(tile_rows, tile_cols, padded_rows, padded_cols)]
    all_to_all x0 -> x2, blocking collectives: none -> 32.6 us  [the longest x1 18.2 us: shards(): blocks = lax.all_to_all(packed, 'row', 0, 0)]
    pallas_call x0 -> x4, Pallas kernels: none -> 18.9 us  [the longest x1 12.8 us: main(): pl.pallas_call(main_kernel, out_shape=(halo, jax.ShapeDtypeStruct((8, 128...]
    ppermute x8 -> x4, starting transfers between devices: 27.7 us -> 12.8 us  [the longest x1 3.9 us: shards(): from_right = lax.ppermute(blocks[:, 128:192], 'col', leftward)]
    all_to_all x0 -> x1, starting transfers between devices: none -> 10.8 us  [shards(): bias_parts = lax.all_to_all(bias_part, 'col', 0, 0)]
    while x19 -> x0, local copies, waits for them, and re-layouts: 10.1 us -> none  [the longest x3 5.77 us: run_queries(): return lax.fori_loop(0, head_count, query_pass, initial)]
  transfers between devices with their start and end apart: 8 -> 5, of which waited for: 6 -> 4; matrix products, arithmetic and copies ran while one was open for 1% -> 0% of each run, Pallas kernels for 0% -> 0%
where the time goes in v1:
time: 85.1 us; the launch traced here: 84.5 us
  blocking collectives  32.6 us (38%)
  starting transfers between devices  23.6 us (28%)
  Pallas kernels  18.9 us (22%)
  waiting for transfers between devices  6.58 us (8%)
  local copies, waits for them, and re-layouts  2.16 us (3%)
    all_to_all x1, blocking collectives, shards(): blocks = lax.all_to_all(packed, 'row', 0, 0)  18.2 us
    all_to_all x1, blocking collectives, shards(): lax.all_to_all(combine(dq, own, share_left, share_right, bias_parts), 'ro...  14.5 us
    pallas_call x1, Pallas kernels, main(): pl.pallas_call(main_kernel, out_shape=(halo, jax.ShapeDtypeStruct((8, 128...  12.8 us
    all_to_all x1, starting transfers between devices, shards(): bias_parts = lax.all_to_all(bias_part, 'col', 0, 0)  10.8 us
    ppermute x1, waiting for transfers between devices, shards(): share_right = lax.ppermute(out_left, 'col', leftward)  4.05 us
    ppermute x1, starting transfers between devices, shards(): from_right = lax.ppermute(blocks[:, 128:192], 'col', leftward)  3.9 us
    ppermute x1, starting transfers between devices, shards(): share_left = lax.ppermute(out_right, 'col', rightward)  3.54 us
    ppermute x1, starting transfers between devices, shards(): from_left = lax.ppermute(blocks[:, 192:256], 'col', rightward)  3.44 us
  transfers between devices with their start and end apart: 5, of which 4 were waited for; matrix products, arithmetic and copies ran while one was open for 0% of the time, Pallas kernels for 0%

profile of v1, /device:TPU:1, one launch (start us, length us, event | category | flops | bytes accessed | tf_op | source)
XLA Modules:
  0.0 84.5 jit_solution(10062217926409439075)
XLA Ops:
  0.6 2.1 %pack.1 = bf16[8,256,128]{2,1,0:T(8,128)(2,1)} custom-call(bf16[8,16,512]{2,1,0:T(8,128)(2,1)} %q_ref.1, bf16[8,16,512]{2,1,0:T(8,128)(2,1)} %k_ref.1, bf16[8,16,512]{2,1,0:T(8,128)(2,1)} %v_ref.1, bf16[8,16,512]{2,1,0:T(8,128)(2,1)} %g_ref.1), custom_call_target="tpu_custom_call" | custom-call | tf_op jit(solution)/shard_map/pack/pallas_call | solution.py:50
  2.7 18.2 %all_to_all.15.x_ref = bf16[8,256,128]{2,1,0:T(8,128)(2,1)S(1)} all-to-all(bf16[8,256,128]{2,1,0:T(8,128)(2,1)} %pack.1), channel_id=1, replica_groups=mesh['row'=8,'col'=32] {'row'}, dimensions={0} | all-to-all | bytes 1048576 | tf_op jit(solution)/shard_map/all_to_all | solution.py:320
  20.9 0.0 copy-start.2
  20.9 0.0 copy-start.3
  20.9 3.9 %collective-permute-start.1 = (bf16[8,64,128]{2,1,0:T(8,128)(2,1)S(1)}, bf16[8,64,128]{2,1,0:T(8,128)(2,1)S(1)}, u32[]{:S(2)}, u32[]{:S(2)}) collective-permute-start(bf16[8,64,128]{2,1,0:T(8,128)(2,1)S(1)} %get-tuple-element.22), channel_id=1, source_target_pairs={{1,0},{2,1},{3,2},{4,3},{5,4},{6,5},{7,6},{8,7},{9,8},{10,9},{11,1... | collective-permute-start | bytes 393224 | tf_op jit(solution)/shard_map/ppermute | solution.py:322
  24.8 3.4 %collective-permute-start = (bf16[8,64,128]{2,1,0:T(8,128)(2,1)S(1)}, bf16[8,64,128]{2,1,0:T(8,128)(2,1)S(1)}, u32[]{:S(2)}, u32[]{:S(2)}) collective-permute-start(bf16[8,64,128]{2,1,0:T(8,128)(2,1)S(1)} %get-tuple-element.23), channel_id=1, source_target_pairs={{0,1},{1,2},{2,3},{3,4},{4,5},{5,6},{6,7},{7,8},{8,9},{9,10},{10,1... | collective-permute-start | bytes 393224 | tf_op jit(solution)/shard_map/ppermute | solution.py:321
  28.3 0.7 collective-permute-done.1.right_ref
  29.0 1.2 %collective-permute-done.left_ref = bf16[8,64,128]{2,1,0:T(8,128)(2,1)S(1)} collective-permute-done((bf16[8,64,128]{2,1,0:T(8,128)(2,1)S(1)}, bf16[8,64,128]{2,1,0:T(8,128)(2,1)S(1)}, u32[]{:S(2)}, u32[]{:S(2)}) %collective-permute-start) | collective-permute-done | bytes 131104 | tf_op jit(solution)/shard_map/ppermute | solution.py:321
  30.2 0.0 copy-done.2
  30.2 0.0 copy-done.3
  30.2 12.8 %attention_backward.1 = (bf16[8,64,128]{2,1,0:T(8,128)(2,1)S(1)}, f32[8,128,128]{2,1,0:T(8,128)S(1)}, bf16[8,64,128]{2,1,0:T(8,128)(2,1)S(1)}, bf16[8,64,128]{2,1,0:T(8,128)(2,1)S(1)}, f32[32,8,128]{2,1,0:T(8,128)}) custom-call(s32[8,32]{1,0:T(8,128)S(1)} %copy-done.3, f32[17,8,17]{2,1,0:T(8,128)S(1)} %bitcast.2, bf16[8,256,128]{2,1,0:T(8,128)(2,1)S(1)} %all_to_all.15.x_ref, ...), custom_call_target="tpu_custom_call" | custom-call | tf_op jit(solution)/shard_map/attention_backward/pallas_call | solution.py:224
  43.1 0.0 copy-start
  43.1 0.8 copy-done
  43.8 0.0 copy-start.1
  43.8 0.7 copy-done.1
  44.5 10.8 %all-to-all-start.1 = ((f32[32,8,128]{2,1,0:T(8,128)}), f32[32,8,128]{2,1,0:T(8,128)S(1)}, u32[]{:S(2)}, u32[]{:S(2)}) async-start(f32[32,8,128]{2,1,0:T(8,128)} %get-tuple-element.17), calls=%async_computation.1 | async-start | bytes 262144 | tf_op jit(solution)/shard_map/all_to_all | solution.py:329
  55.3 3.5 %collective-permute-start.2 = (bf16[8,64,128]{2,1,0:T(8,128)(2,1)S(1)}, bf16[8,64,128]{2,1,0:T(8,128)(2,1)S(1)}, u32[]{:S(2)}, u32[]{:S(2)}) collective-permute-start(bf16[8,64,128]{2,1,0:T(8,128)(2,1)S(1)} %get-tuple-element.15), channel_id=1, source_target_pairs={{0,1},{1,2},{2,3},{3,4},{4,5},{5,6},{6,7},{7,8},{8,9},{9,10},{10,1... | collective-permute-start | bytes 393224 | tf_op jit(solution)/shard_map/ppermute | solution.py:327
  58.8 1.9 %collective-permute-start.3 = (bf16[8,64,128]{2,1,0:T(8,128)(2,1)S(1)}, bf16[8,64,128]{2,1,0:T(8,128)(2,1)S(1)}, u32[]{:S(2)}, u32[]{:S(2)}) collective-permute-start(bf16[8,64,128]{2,1,0:T(8,128)(2,1)S(1)} %get-tuple-element.16), channel_id=1, source_target_pairs={{1,0},{2,1},{3,2},{4,3},{5,4},{6,5},{7,6},{8,7},{9,8},{10,9},{11,1... | collective-permute-start | bytes 393224 | tf_op jit(solution)/shard_map/ppermute | solution.py:328
  60.8 0.6 collective-permute-done.2.left_ref
  61.4 0.0 copy-start.5
  61.4 4.1 %collective-permute-done.3.right_ref = bf16[8,64,128]{2,1,0:T(8,128)(2,1)S(1)} collective-permute-done((bf16[8,64,128]{2,1,0:T(8,128)(2,1)S(1)}, bf16[8,64,128]{2,1,0:T(8,128)(2,1)S(1)}, u32[]{:S(2)}, u32[]{:S(2)}) %collective-permute-start.3) | collective-permute-done | bytes 131104 | tf_op jit(solution)/shard_map/ppermute | solution.py:328
  65.4 0.0 copy-start.6
  65.4 0.0 all-to-all-done.1.bias_ref
  65.4 0.0 copy-start.4
  65.4 0.0 copy-done.5
  65.4 0.6 copy-done.6
  66.1 0.1 copy-done.4
  66.1 2.0 %combine.1 = bf16[8,224,128]{2,1,0:T(8,128)(2,1)} custom-call(bf16[8,64,128]{2,1,0:T(8,128)(2,1)} %copy-done.1, f32[8,128,128]{2,1,0:T(8,128)} %copy-done, bf16[8,64,128]{2,1,0:T(8,128)(2,1)} %copy-done.5, bf16[8,64,128]{2,1,0:T(8,128)(2,1)} %copy-done.6, f32[32,8,128]{2,1,0:T(8,128)} %copy-done.4), custom_call_target="tpu_custom_call" | custom-call | tf_op jit(solution)/shard_map/combine/pallas_call | solution.py:266
  68.1 14.5 %all_to_all.16.z_ref = bf16[8,224,128]{2,1,0:T(8,128)(2,1)} all-to-all(bf16[8,224,128]{2,1,0:T(8,128)(2,1)} %combine.1), channel_id=1, replica_groups=mesh['row'=8,'col'=32] {'row'}, dimensions={0} | all-to-all | bytes 917504 | tf_op jit(solution)/shard_map/all_to_all | solution.py:330
  82.6 2.0 %unpack.1 = (bf16[8,16,512]{2,1,0:T(8,128)(2,1)}, bf16[8,16,512]{2,1,0:T(8,128)(2,1)}, bf16[8,16,512]{2,1,0:T(8,128)(2,1)}, f32[17,8,17]{2,1,0:T(8,128)}) custom-call(bf16[8,224,128]{2,1,0:T(8,128)(2,1)} %all_to_all.16.z_ref), custom_call_target="tpu_custom_call" | custom-call | tf_op jit(solution)/shard_map/unpack/pallas_call | solution.py:305
  (1 shorter events, 0.0 us)
Async XLA Ops:
  20.9 9.3 %copy-start.2 = (f32[8,17,17]{2,0,1:T(8,128)S(1)}, f32[8,17,17]{2,0,1:T(8,128)}, u32[]{:S(2)}) copy-start(f32[8,17,17]{2,0,1:T(8,128)} %param.10) | copy-start | bytes 27748
  20.9 9.3 %copy-start.3 = (s32[8,32]{1,0:T(8,128)S(1)}, s32[8,32]{1,0:T(8,128)}, u32[]{:S(2)}) copy-start(s32[8,32]{1,0:T(8,128)} %occ_ref.1) | copy-start | bytes 3076
  20.9 8.1 %collective-permute-start.1 = (bf16[8,64,128]{2,1,0:T(8,128)(2,1)S(1)}, bf16[8,64,128]{2,1,0:T(8,128)(2,1)S(1)}, u32[]{:S(2)}, u32[]{:S(2)}) collective-permute-start(bf16[8,64,128]{2,1,0:T(8,128)(2,1)S(1)} %get-tuple-element.22), channel_id=1, source_target_pairs={{1,0},{2,1},{3,2},{4,3},{5,4},{6,5},{7,6},{8,7},{9,8},{10,9},{11,1... | collective-permute-start | bytes 393224 | tf_op jit(solution)/shard_map/ppermute | solution.py:322
  24.8 5.4 %collective-permute-start = (bf16[8,64,128]{2,1,0:T(8,128)(2,1)S(1)}, bf16[8,64,128]{2,1,0:T(8,128)(2,1)S(1)}, u32[]{:S(2)}, u32[]{:S(2)}) collective-permute-start(bf16[8,64,128]{2,1,0:T(8,128)(2,1)S(1)} %get-tuple-element.23), channel_id=1, source_target_pairs={{0,1},{1,2},{2,3},{3,4},{4,5},{5,6},{6,7},{7,8},{8,9},{9,10},{10,1... | collective-permute-start | bytes 393224 | tf_op jit(solution)/shard_map/ppermute | solution.py:321
  43.1 0.8 copy-start
  43.8 0.7 copy-start.1
  44.5 20.9 %all-to-all-start.1 = ((f32[32,8,128]{2,1,0:T(8,128)}), f32[32,8,128]{2,1,0:T(8,128)S(1)}, u32[]{:S(2)}, u32[]{:S(2)}) async-start(f32[32,8,128]{2,1,0:T(8,128)} %get-tuple-element.17), calls=%async_computation.1 | async-start | bytes 262144 | tf_op jit(solution)/shard_map/all_to_all | solution.py:329
  55.3 6.1 %collective-permute-start.2 = (bf16[8,64,128]{2,1,0:T(8,128)(2,1)S(1)}, bf16[8,64,128]{2,1,0:T(8,128)(2,1)S(1)}, u32[]{:S(2)}, u32[]{:S(2)}) collective-permute-start(bf16[8,64,128]{2,1,0:T(8,128)(2,1)S(1)} %get-tuple-element.15), channel_id=1, source_target_pairs={{0,1},{1,2},{2,3},{3,4},{4,5},{5,6},{6,7},{7,8},{8,9},{9,10},{10,1... | collective-permute-start | bytes 393224 | tf_op jit(solution)/shard_map/ppermute | solution.py:327
  58.8 6.6 %collective-permute-start.3 = (bf16[8,64,128]{2,1,0:T(8,128)(2,1)S(1)}, bf16[8,64,128]{2,1,0:T(8,128)(2,1)S(1)}, u32[]{:S(2)}, u32[]{:S(2)}) collective-permute-start(bf16[8,64,128]{2,1,0:T(8,128)(2,1)S(1)} %get-tuple-element.16), channel_id=1, source_target_pairs={{1,0},{2,1},{3,2},{4,3},{5,4},{6,5},{7,6},{8,7},{9,8},{10,9},{11,1... | collective-permute-start | bytes 393224 | tf_op jit(solution)/shard_map/ppermute | solution.py:328
  61.4 4.1 %copy-start.5 = (bf16[8,64,128]{2,1,0:T(8,128)(2,1)}, bf16[8,64,128]{2,1,0:T(8,128)(2,1)S(1)}, u32[]{:S(2)}) copy-start(bf16[8,64,128]{2,1,0:T(8,128)(2,1)S(1)} %collective-permute-done.2.left_ref) | copy-start | bytes 393220
  65.4 0.6 copy-start.6
  65.4 0.7 copy-start.4

commit v2 on v1

--- a/solution.py
+++ b/solution.py
@@ -133,50 +133,52 @@
     col = lax.axis_index("col")
     col_count = occ_ref.shape[1]
     build_table(head, bias_ref, rows_ref, table_ref)
+    low = lanes_of((128, 128)) < 64
     sums_ref[...] = jnp.zeros_like(sums_ref)
-    for edge in (0, 9):
-        kv_ref[edge] = jnp.zeros((256, 128), jnp.bfloat16)
-        kt_ref[edge] = jnp.zeros((128, 256), jnp.bfloat16)
-        qg_ref[edge] = jnp.zeros((256, 128), jnp.bfloat16)
-    p_ref[1, :, 0:256] = jnp.zeros((256, 256), jnp.bfloat16)
-    p_ref[8, :, 512:768] = jnp.zeros((256, 256), jnp.bfloat16)
-    low = lanes_of((128, 128)) < 64
-
-    def stage(j, carry):
-        kv_ref[j + 1, 0:64] = left_ref[j]
-        kv_ref[j + 1, 64:192] = x_ref[j, 128:256]
-        kv_ref[j + 1, 192:256] = right_ref[j]
-        kt_ref[j + 1] = jnp.transpose(kv_ref[j + 1].astype(jnp.float32)).astype(jnp.bfloat16)
-        query_grad = x_ref[j, 0:128].astype(jnp.float32)
-        qg_ref[j + 1, 0:128] = jnp.where(low, query_grad, 0.0).astype(jnp.bfloat16)
-        qg_ref[j + 1, 128:256] = jnp.where(low, 0.0, query_grad).astype(jnp.bfloat16)
-        return carry
-
-    lax.fori_loop(0, 8, stage, 0)
 
     def filled(row, at):
-        inside = (row >= 0) & (row < 8) & (at >= 0) & (at < col_count)
-        value = occ_ref[jnp.clip(row, 0, 7), jnp.clip(at, 0, col_count - 1)]
-        return inside & (value > 0)
+        inside = (at >= 0) & (at < col_count)
+        return inside & (occ_ref[row, jnp.clip(at, 0, col_count - 1)] > 0)
 
     def penalty(row, at):
         return jnp.where(filled(row, at), jnp.float32(0.0), jnp.float32(MASKED))
 
-    def tile(i, carry):
-        keys = kv_ref[pl.ds(i, 3)].reshape(768, 128)
-        both = lax.dot_general(
-            keys, qg_ref[i + 1], (((1,), (1,)), ((), ())), preferred_element_type=jnp.float32
+    marks = []
+    for j in range(8):
+        kv_ref[256 * j : 256 * j + 64] = left_ref[j]
+        kv_ref[256 * j + 64 : 256 * j + 192] = x_ref[j, 128:256]
+        kv_ref[256 * j + 192 : 256 * j + 256] = right_ref[j]
+        flipped = jnp.transpose(kv_ref[256 * j : 256 * j + 256])
+        kt_ref[:, 256 * j : 256 * j + 256] = flipped[0:64]
+        query_grad = x_ref[j, 0:128]
+        zero = jnp.zeros_like(query_grad)
+        qg_ref[256 * j : 256 * j + 128] = jnp.where(low, query_grad, zero)
+        qg_ref[256 * j + 128 : 256 * j + 256] = jnp.where(low, zero, query_grad)
+        own = penalty(j, col)
+        marks.append((penalty(j, col - 1), own, own, penalty(j, col + 1)))
+
+    def window(i):
+        steps = [step for step in range(3) if 0 <= i - 1 + step < 8]
+        return steps, i - 1 + steps[0], len(steps)
+
+    def products(i):
+        _, first, count = window(i)
+        return lax.dot_general(
+            kv_ref[256 * first : 256 * (first + count)],
+            qg_ref[256 * i : 256 * i + 256],
+            (((1,), (1,)), ((), ())),
+            preferred_element_type=jnp.float32,
         )
+
+    def softmax(i, both):
+        steps, first, count = window(i)
         scores, grads = both[:, 0:128], both[:, 128:256]
         shifted = []
-        for step in range(3):
-            row = i - 1 + step
-            own = penalty(row, col)
-            marks = (penalty(row, col - 1), own, own, penalty(row, col + 1))
+        for step in steps:
             for chunk in range(4):
-                at = 256 * step + 64 * chunk
-                bias = table_ref[step, chunk].reshape(64, 128)
-                shifted.append(scores[at : at + 64] * LOG2E + (bias + marks[chunk]))
+                at = 256 * (step - steps[0]) + 64 * chunk
+                bias = table_ref[step, chunk].reshape(64, 128) + marks[i - 1 + step][chunk]
+                shifted.append(scores[at : at + 64] * LOG2E + bias)
         shifted = jnp.concatenate(shifted, axis=0)
         top = jnp.max(shifted, axis=0, keepdims=True)
         exponent = jnp.exp2(shifted - top)
@@ -187,35 +189,39 @@
         used = jnp.where(filled(i, col), jnp.float32(1.0), jnp.float32(0.0))
         weights = exponent * (inverse * used)
         grad_scores = weights * (grads - delta)
-        sums_ref[...] += grad_scores.reshape(3, 4, 8, 8, 128)
-        weights_low = weights.astype(jnp.bfloat16)
-        grad_low = grad_scores.astype(jnp.bfloat16)
-        grad_query = jnp.zeros((128, 128), jnp.float32)
-        for step in range(3):
-            part = grad_low[256 * step : 256 * step + 256]
-            slot = 256 * (2 - step)
-            p_ref[i + step, :, slot : slot + 128] = part
-            p_ref[i + step, :, slot + 128 : slot + 256] = weights_low[256 * step : 256 * step + 256]
-            grad_query += jnp.dot(kt_ref[i + step], part, preferred_element_type=jnp.float32)
-        grad_query = jnp.transpose(grad_query * 0.125)
-        packed = jnp.where(low[0:64], grad_query[0:64], swap_halves(grad_query[64:128]))
-        dq_ref[i] = packed.astype(jnp.bfloat16)
-        return carry
-
-    lax.fori_loop(0, 8, tile, 0)
-
-    def keys_pass(j, carry):
-        result = jnp.dot(
-            p_ref[j + 1],
-            qg_ref[pl.ds(j, 3)].reshape(768, 128),
+        sums_ref[steps[0] : steps[-1] + 1] += grad_scores.reshape(count, 4, 8, 8, 128)
+        return weights.astype(jnp.bfloat16), grad_scores.astype(jnp.bfloat16)
+
+    def gradients(i, weights_low, grad_low):
+        steps, first, count = window(i)
+        shares = jnp.dot(
+            jnp.concatenate([grad_low, weights_low], axis=1),
+            qg_ref[256 * i : 256 * i + 256],
             preferred_element_type=jnp.float32,
         )
-        out_left_ref[j] = result[0:64].astype(jnp.bfloat16)
-        own_ref[j] = result[64:192]
-        out_right_ref[j] = result[192:256].astype(jnp.bfloat16)
-        return carry
-
-    lax.fori_loop(0, 8, keys_pass, 0)
+        grad_query = jnp.dot(
+            kt_ref[:, 256 * first : 256 * (first + count)],
+            grad_low,
+            preferred_element_type=jnp.float32,
+        )
+        dq_ref[i] = (grad_query * 0.125).astype(jnp.bfloat16)
+        for step in steps:
+            at = 256 * (step - steps[0])
+            j = i - 1 + step
+            part = shares[at : at + 256]
+            if not (step == 2 or i == 0):
+                part = part + p_ref[j]
+            if step == 0 or i == 7:
+                out_left_ref[j] = part[0:64].astype(jnp.bfloat16)
+                own_ref[j] = part[64:192]
+                out_right_ref[j] = part[192:256].astype(jnp.bfloat16)
+            else:
+                p_ref[j] = part
+
+    both = {i: products(i) for i in range(8)}
+    pairs = [softmax(i, both[i]) for i in range(8)]
+    for i in range(8):
+        gradients(i, *pairs[i])
     contract_bias(sums_ref, skew_ref, bias_out_ref)
 
 
@@ -237,10 +243,10 @@
             pltpu.VMEM((3, 4, 8, 8, 128), jnp.float32),
             pltpu.VMEM((3, 4, 8, 8, 128), jnp.float32),
             pltpu.VMEM((17, 4, 8, 128), jnp.float32),
-            pltpu.VMEM((10, 256, 128), jnp.bfloat16),
-            pltpu.VMEM((10, 128, 256), jnp.bfloat16),
-            pltpu.VMEM((10, 256, 128), jnp.bfloat16),
-            pltpu.VMEM((10, 256, 768), jnp.bfloat16),
+            pltpu.VMEM((2048, 128), jnp.bfloat16),
+            pltpu.VMEM((64, 2048), jnp.bfloat16),
+            pltpu.VMEM((2048, 128), jnp.bfloat16),
+            pltpu.VMEM((8, 256, 128), jnp.float32),
         ],
         compiler_params=pltpu.CompilerParams(vmem_limit_bytes=40 << 20),
         name="attention_backward",
@@ -283,9 +289,7 @@
         lanes = pl.ds(128 * pair, 128)
         even = z_ref[2 * pair].astype(jnp.float32)
         odd = z_ref[2 * pair + 1].astype(jnp.float32)
-        first = jnp.where(low[0:64], even[0:64], swap_halves(odd[0:64]))
-        second = jnp.where(low[0:64], swap_halves(even[0:64]), odd[0:64])
-        query = jnp.concatenate([first, second], axis=0)
+        query = jnp.transpose(jnp.concatenate([even[0:64], odd[0:64]], axis=0))
         gq_ref[:, :, lanes] = query.reshape(8, 16, 128).astype(jnp.bfloat16)
         key = jnp.where(low, even[64:192], swap_halves(odd[64:192]))
         value = jnp.where(low, swap_halves(even[64:192]), odd[64:192])

time: 85.1 us -> 76.5 us (0.90)
  Pallas kernels: 18.9 us -> 10.3 us
    pallas_call x1, Pallas kernels: 12.8 us -> 4.27 us  [main(): pl.pallas_call(main_kernel, out_shape=(halo, jax.ShapeDtypeStruct((8, 128...]
where the time goes in v2:
time: 76.5 us; the launch traced here: 75.9 us
  blocking collectives  32.6 us (43%)
  starting transfers between devices  23.6 us (31%)
  Pallas kernels  10.3 us (13%)
  waiting for transfers between devices  6.58 us (9%)
  local copies, waits for them, and re-layouts  2.16 us (3%)
    all_to_all x1, blocking collectives, shards(): blocks = lax.all_to_all(packed, 'row', 0, 0)  18.2 us
    all_to_all x1, blocking collectives, shards(): lax.all_to_all(combine(dq, own, share_left, share_right, bias_parts), 'ro...  14.5 us
    all_to_all x1, starting transfers between devices, shards(): bias_parts = lax.all_to_all(bias_part, 'col', 0, 0)  10.8 us
    pallas_call x1, Pallas kernels, main(): pl.pallas_call(main_kernel, out_shape=(halo, jax.ShapeDtypeStruct((8, 128...  4.27 us
    ppermute x1, waiting for transfers between devices, shards(): share_right = lax.ppermute(out_left, 'col', leftward)  4.05 us
    ppermute x1, starting transfers between devices, shards(): from_right = lax.ppermute(blocks[:, 128:192], 'col', leftward)  3.9 us
    ppermute x1, starting transfers between devices, shards(): share_left = lax.ppermute(out_right, 'col', rightward)  3.54 us
    ppermute x1, starting transfers between devices, shards(): from_left = lax.ppermute(blocks[:, 192:256], 'col', rightward)  3.44 us
  transfers between devices with their start and end apart: 5, of which 4 were waited for; matrix products, arithmetic and copies ran while one was open for 0% of the time, Pallas kernels for 0%

profile of v2, /device:TPU:1, one launch (start us, length us, event | category | flops | bytes accessed | tf_op | source)
XLA Modules:
  0.0 75.9 jit_solution(11850642614390827249)
XLA Ops:
  0.6 2.1 %pack.1 = bf16[8,256,128]{2,1,0:T(8,128)(2,1)} custom-call(bf16[8,16,512]{2,1,0:T(8,128)(2,1)} %q_ref.1, bf16[8,16,512]{2,1,0:T(8,128)(2,1)} %k_ref.1, bf16[8,16,512]{2,1,0:T(8,128)(2,1)} %v_ref.1, bf16[8,16,512]{2,1,0:T(8,128)(2,1)} %g_ref.1), custom_call_target="tpu_custom_call" | custom-call | tf_op jit(solution)/shard_map/pack/pallas_call | solution.py:50
  2.7 18.2 %all_to_all.15.x_ref = bf16[8,256,128]{2,1,0:T(8,128)(2,1)S(1)} all-to-all(bf16[8,256,128]{2,1,0:T(8,128)(2,1)} %pack.1), channel_id=1, replica_groups=mesh['row'=8,'col'=32] {'row'}, dimensions={0} | all-to-all | bytes 1048576 | tf_op jit(solution)/shard_map/all_to_all | solution.py:324
  20.9 0.0 copy-start.2
  20.9 0.0 copy-start.3
  20.9 3.9 %collective-permute-start.1 = (bf16[8,64,128]{2,1,0:T(8,128)(2,1)S(1)}, bf16[8,64,128]{2,1,0:T(8,128)(2,1)S(1)}, u32[]{:S(2)}, u32[]{:S(2)}) collective-permute-start(bf16[8,64,128]{2,1,0:T(8,128)(2,1)S(1)} %get-tuple-element.22), channel_id=1, source_target_pairs={{1,0},{2,1},{3,2},{4,3},{5,4},{6,5},{7,6},{8,7},{9,8},{10,9},{11,1... | collective-permute-start | bytes 393224 | tf_op jit(solution)/shard_map/ppermute | solution.py:326
  24.8 3.4 %collective-permute-start = (bf16[8,64,128]{2,1,0:T(8,128)(2,1)S(1)}, bf16[8,64,128]{2,1,0:T(8,128)(2,1)S(1)}, u32[]{:S(2)}, u32[]{:S(2)}) collective-permute-start(bf16[8,64,128]{2,1,0:T(8,128)(2,1)S(1)} %get-tuple-element.23), channel_id=1, source_target_pairs={{0,1},{1,2},{2,3},{3,4},{4,5},{5,6},{6,7},{7,8},{8,9},{9,10},{10,1... | collective-permute-start | bytes 393224 | tf_op jit(solution)/shard_map/ppermute | solution.py:325
  28.3 0.7 collective-permute-done.1.right_ref
  29.0 1.2 %collective-permute-done.left_ref = bf16[8,64,128]{2,1,0:T(8,128)(2,1)S(1)} collective-permute-done((bf16[8,64,128]{2,1,0:T(8,128)(2,1)S(1)}, bf16[8,64,128]{2,1,0:T(8,128)(2,1)S(1)}, u32[]{:S(2)}, u32[]{:S(2)}) %collective-permute-start) | collective-permute-done | bytes 131104 | tf_op jit(solution)/shard_map/ppermute | solution.py:325
  30.2 0.0 copy-done.2
  30.2 0.0 copy-done.3
  30.2 4.3 %attention_backward.1 = (bf16[8,64,128]{2,1,0:T(8,128)(2,1)S(1)}, f32[8,128,128]{2,1,0:T(8,128)S(1)}, bf16[8,64,128]{2,1,0:T(8,128)(2,1)S(1)}, bf16[8,64,128]{2,1,0:T(8,128)(2,1)S(1)}, f32[32,8,128]{2,1,0:T(8,128)}) custom-call(s32[8,32]{1,0:T(8,128)S(1)} %copy-done.3, f32[17,8,17]{2,1,0:T(8,128)S(1)} %bitcast.2, bf16[8,256,128]{2,1,0:T(8,128)(2,1)S(1)} %all_to_all.15.x_ref, ...), custom_call_target="tpu_custom_call" | custom-call | tf_op jit(solution)/shard_map/attention_backward/pallas_call | solution.py:230
  34.5 0.0 copy-start
  34.5 0.8 %copy-done = f32[8,128,128]{2,1,0:T(8,128)} copy-done((f32[8,128,128]{2,1,0:T(8,128)}, f32[8,128,128]{2,1,0:T(8,128)S(1)}, u32[]{:S(2)}) %copy-start) | copy-done | bytes 524312
  35.3 0.0 copy-start.1
  35.3 0.7 copy-done.1
  35.9 10.8 %all-to-all-start.1 = ((f32[32,8,128]{2,1,0:T(8,128)}), f32[32,8,128]{2,1,0:T(8,128)S(1)}, u32[]{:S(2)}, u32[]{:S(2)}) async-start(f32[32,8,128]{2,1,0:T(8,128)} %get-tuple-element.17), calls=%async_computation.1 | async-start | bytes 262144 | tf_op jit(solution)/shard_map/all_to_all | solution.py:333
  46.7 3.5 %collective-permute-start.2 = (bf16[8,64,128]{2,1,0:T(8,128)(2,1)S(1)}, bf16[8,64,128]{2,1,0:T(8,128)(2,1)S(1)}, u32[]{:S(2)}, u32[]{:S(2)}) collective-permute-start(bf16[8,64,128]{2,1,0:T(8,128)(2,1)S(1)} %get-tuple-element.15), channel_id=1, source_target_pairs={{0,1},{1,2},{2,3},{3,4},{4,5},{5,6},{6,7},{7,8},{8,9},{9,10},{10,1... | collective-permute-start | bytes 393224 | tf_op jit(solution)/shard_map/ppermute | solution.py:331
  50.3 1.9 %collective-permute-start.3 = (bf16[8,64,128]{2,1,0:T(8,128)(2,1)S(1)}, bf16[8,64,128]{2,1,0:T(8,128)(2,1)S(1)}, u32[]{:S(2)}, u32[]{:S(2)}) collective-permute-start(bf16[8,64,128]{2,1,0:T(8,128)(2,1)S(1)} %get-tuple-element.16), channel_id=1, source_target_pairs={{1,0},{2,1},{3,2},{4,3},{5,4},{6,5},{7,6},{8,7},{9,8},{10,9},{11,1... | collective-permute-start | bytes 393224 | tf_op jit(solution)/shard_map/ppermute | solution.py:332
  52.2 0.6 collective-permute-done.2.left_ref
  52.8 0.0 copy-start.5
  52.8 4.1 %collective-permute-done.3.right_ref = bf16[8,64,128]{2,1,0:T(8,128)(2,1)S(1)} collective-permute-done((bf16[8,64,128]{2,1,0:T(8,128)(2,1)S(1)}, bf16[8,64,128]{2,1,0:T(8,128)(2,1)S(1)}, u32[]{:S(2)}, u32[]{:S(2)}) %collective-permute-start.3) | collective-permute-done | bytes 131104 | tf_op jit(solution)/shard_map/ppermute | solution.py:332
  56.9 0.0 copy-start.6
  56.9 0.0 all-to-all-done.1.bias_ref
  56.9 0.0 copy-start.4
  56.9 0.0 copy-done.5
  56.9 0.6 copy-done.6
  57.5 0.1 copy-done.4
  57.5 2.0 %combine.1 = bf16[8,224,128]{2,1,0:T(8,128)(2,1)} custom-call(bf16[8,64,128]{2,1,0:T(8,128)(2,1)} %copy-done.1, f32[8,128,128]{2,1,0:T(8,128)} %copy-done, bf16[8,64,128]{2,1,0:T(8,128)(2,1)} %copy-done.5, bf16[8,64,128]{2,1,0:T(8,128)(2,1)} %copy-done.6, f32[32,8,128]{2,1,0:T(8,128)} %copy-done.4), custom_call_target="tpu_custom_call" | custom-call | tf_op jit(solution)/shard_map/combine/pallas_call | solution.py:272
  59.5 14.5 %all_to_all.16.z_ref = bf16[8,224,128]{2,1,0:T(8,128)(2,1)} all-to-all(bf16[8,224,128]{2,1,0:T(8,128)(2,1)} %combine.1), channel_id=1, replica_groups=mesh['row'=8,'col'=32] {'row'}, dimensions={0} | all-to-all | bytes 917504 | tf_op jit(solution)/shard_map/all_to_all | solution.py:334
  74.0 1.9 %unpack.1 = (bf16[8,16,512]{2,1,0:T(8,128)(2,1)}, bf16[8,16,512]{2,1,0:T(8,128)(2,1)}, bf16[8,16,512]{2,1,0:T(8,128)(2,1)}, f32[17,8,17]{2,1,0:T(8,128)}) custom-call(bf16[8,224,128]{2,1,0:T(8,128)(2,1)} %all_to_all.16.z_ref), custom_call_target="tpu_custom_call" | custom-call | tf_op jit(solution)/shard_map/unpack/pallas_call | solution.py:309
  (1 shorter events, 0.0 us)
Async XLA Ops:
  20.9 9.3 %copy-start.2 = (f32[8,17,17]{2,0,1:T(8,128)S(1)}, f32[8,17,17]{2,0,1:T(8,128)}, u32[]{:S(2)}) copy-start(f32[8,17,17]{2,0,1:T(8,128)} %param.10) | copy-start | bytes 27748
  20.9 9.3 %copy-start.3 = (s32[8,32]{1,0:T(8,128)S(1)}, s32[8,32]{1,0:T(8,128)}, u32[]{:S(2)}) copy-start(s32[8,32]{1,0:T(8,128)} %occ_ref.1) | copy-start | bytes 3076
  20.9 8.1 %collective-permute-start.1 = (bf16[8,64,128]{2,1,0:T(8,128)(2,1)S(1)}, bf16[8,64,128]{2,1,0:T(8,128)(2,1)S(1)}, u32[]{:S(2)}, u32[]{:S(2)}) collective-permute-start(bf16[8,64,128]{2,1,0:T(8,128)(2,1)S(1)} %get-tuple-element.22), channel_id=1, source_target_pairs={{1,0},{2,1},{3,2},{4,3},{5,4},{6,5},{7,6},{8,7},{9,8},{10,9},{11,1... | collective-permute-start | bytes 393224 | tf_op jit(solution)/shard_map/ppermute | solution.py:326
  24.8 5.4 %collective-permute-start = (bf16[8,64,128]{2,1,0:T(8,128)(2,1)S(1)}, bf16[8,64,128]{2,1,0:T(8,128)(2,1)S(1)}, u32[]{:S(2)}, u32[]{:S(2)}) collective-permute-start(bf16[8,64,128]{2,1,0:T(8,128)(2,1)S(1)} %get-tuple-element.23), channel_id=1, source_target_pairs={{0,1},{1,2},{2,3},{3,4},{4,5},{5,6},{6,7},{7,8},{8,9},{9,10},{10,1... | collective-permute-start | bytes 393224 | tf_op jit(solution)/shard_map/ppermute | solution.py:325
  34.5 0.8 %copy-start = (f32[8,128,128]{2,1,0:T(8,128)}, f32[8,128,128]{2,1,0:T(8,128)S(1)}, u32[]{:S(2)}) copy-start(f32[8,128,128]{2,1,0:T(8,128)S(1)} %get-tuple-element.14.own_ref) | copy-start | bytes 1572868
  35.3 0.7 copy-start.1
  35.9 20.9 %all-to-all-start.1 = ((f32[32,8,128]{2,1,0:T(8,128)}), f32[32,8,128]{2,1,0:T(8,128)S(1)}, u32[]{:S(2)}, u32[]{:S(2)}) async-start(f32[32,8,128]{2,1,0:T(8,128)} %get-tuple-element.17), calls=%async_computation.1 | async-start | bytes 262144 | tf_op jit(solution)/shard_map/all_to_all | solution.py:333
  46.7 6.1 %collective-permute-start.2 = (bf16[8,64,128]{2,1,0:T(8,128)(2,1)S(1)}, bf16[8,64,128]{2,1,0:T(8,128)(2,1)S(1)}, u32[]{:S(2)}, u32[]{:S(2)}) collective-permute-start(bf16[8,64,128]{2,1,0:T(8,128)(2,1)S(1)} %get-tuple-element.15), channel_id=1, source_target_pairs={{0,1},{1,2},{2,3},{3,4},{4,5},{5,6},{6,7},{7,8},{8,9},{9,10},{10,1... | collective-permute-start | bytes 393224 | tf_op jit(solution)/shard_map/ppermute | solution.py:331
  50.3 6.6 %collective-permute-start.3 = (bf16[8,64,128]{2,1,0:T(8,128)(2,1)S(1)}, bf16[8,64,128]{2,1,0:T(8,128)(2,1)S(1)}, u32[]{:S(2)}, u32[]{:S(2)}) collective-permute-start(bf16[8,64,128]{2,1,0:T(8,128)(2,1)S(1)} %get-tuple-element.16), channel_id=1, source_target_pairs={{1,0},{2,1},{3,2},{4,3},{5,4},{6,5},{7,6},{8,7},{9,8},{10,9},{11,1... | collective-permute-start | bytes 393224 | tf_op jit(solution)/shard_map/ppermute | solution.py:332
  52.8 4.1 %copy-start.5 = (bf16[8,64,128]{2,1,0:T(8,128)(2,1)}, bf16[8,64,128]{2,1,0:T(8,128)(2,1)S(1)}, u32[]{:S(2)}) copy-start(bf16[8,64,128]{2,1,0:T(8,128)(2,1)S(1)} %collective-permute-done.2.left_ref) | copy-start | bytes 393220
  56.9 0.6 copy-start.6
  56.9 0.7 copy-start.4

commit v3 on v2

--- a/solution.py
+++ b/solution.py
@@ -10,6 +10,7 @@
 LOG2E = 1.4426950408889634
 MASKED = -1e30
 VMEM_SPEC = pl.BlockSpec(memory_space=pltpu.VMEM)
+HBM_SPEC = pl.BlockSpec(memory_space=pltpu.HBM)
 SMEM_SPEC = pl.BlockSpec(memory_space=pltpu.SMEM)
 
 
@@ -21,7 +22,17 @@
     return pltpu.roll(array, 64, 1)
 
 
-def pack_kernel(q_ref, k_ref, v_ref, g_ref, out_ref):
+def pack_kernel(q_hbm, k_hbm, v_hbm, g_hbm, out_ref, q_ref, k_ref, v_ref, g_ref, sems):
+    copies = [
+        pltpu.make_async_copy(source, target, sems.at[at])
+        for at, (source, target) in enumerate(
+            ((q_hbm, q_ref), (g_hbm, g_ref), (k_hbm, k_ref), (v_hbm, v_ref))
+        )
+    ]
+    for copy in copies:
+        copy.start()
+    for copy in copies:
+        copy.wait()
     low = lanes_of((128, 128)) < 64
     for pair in range(4):
         lanes = pl.ds(128 * pair, 128)
@@ -50,8 +61,11 @@
     return pl.pallas_call(
         pack_kernel,
         out_shape=jax.ShapeDtypeStruct((8, 256, 128), jnp.bfloat16),
-        in_specs=[VMEM_SPEC] * 4,
+        in_specs=[HBM_SPEC] * 4,
         out_specs=VMEM_SPEC,
+        scratch_shapes=[pltpu.VMEM((8, 16, 512), jnp.bfloat16)] * 4
+        + [pltpu.SemaphoreType.DMA((4,))],
+        compiler_params=pltpu.CompilerParams(vmem_limit_bytes=60 << 20),
         name="pack",
     )(queries, keys, values, grad_out)
 
@@ -103,22 +117,19 @@
         precision=lax.Precision.HIGHEST,
         preferred_element_type=jnp.float32,
     )
-    rows = [total[0:1, 128 * k : 128 * k + 128] for k in range(5)]
-    rows.append(jnp.zeros((3, 128), jnp.float32))
-    block = jnp.concatenate(rows, axis=0)
-    bias_out_ref[...] = jnp.broadcast_to(block[None], bias_out_ref.shape)
+    bias_out_ref[...] = jnp.broadcast_to(total[0:1, :][None], bias_out_ref.shape)
 
 
 def main_kernel(
     occ_ref,
     bias_ref,
     x_ref,
-    left_ref,
-    right_ref,
+    inner_ref,
+    outer_ref,
     dq_ref,
     own_ref,
-    out_left_ref,
-    out_right_ref,
+    out_inner_ref,
+    out_outer_ref,
     bias_out_ref,
     rows_ref,
     table_ref,
@@ -132,6 +143,7 @@
     head = lax.axis_index("row")
     col = lax.axis_index("col")
     col_count = occ_ref.shape[1]
+    even = (col & 1) == 0
     build_table(head, bias_ref, rows_ref, table_ref)
     low = lanes_of((128, 128)) < 64
     sums_ref[...] = jnp.zeros_like(sums_ref)
@@ -145,9 +157,10 @@
 
     marks = []
     for j in range(8):
-        kv_ref[256 * j : 256 * j + 64] = left_ref[j]
+        inner, outer = inner_ref[j], outer_ref[j]
+        kv_ref[256 * j : 256 * j + 64] = jnp.where(even, outer, inner)
         kv_ref[256 * j + 64 : 256 * j + 192] = x_ref[j, 128:256]
-        kv_ref[256 * j + 192 : 256 * j + 256] = right_ref[j]
+        kv_ref[256 * j + 192 : 256 * j + 256] = jnp.where(even, inner, outer)
         flipped = jnp.transpose(kv_ref[256 * j : 256 * j + 256])
         kt_ref[:, 256 * j : 256 * j + 256] = flipped[0:64]
         query_grad = x_ref[j, 0:128]
@@ -212,9 +225,10 @@
             if not (step == 2 or i == 0):
                 part = part + p_ref[j]
             if step == 0 or i == 7:
-                out_left_ref[j] = part[0:64].astype(jnp.bfloat16)
+                left, right = part[0:64], part[192:256]
+                out_inner_ref[j] = jnp.where(even, right, left).astype(jnp.bfloat16)
                 own_ref[j] = part[64:192]
-                out_right_ref[j] = part[192:256].astype(jnp.bfloat16)
+                out_outer_ref[j] = jnp.where(even, left, right).astype(jnp.bfloat16)
             else:
                 p_ref[j] = part
 
@@ -225,7 +239,7 @@
     contract_bias(sums_ref, skew_ref, bias_out_ref)
 
 
-def main(occupied, bias, blocks, left, right, col_count):
+def main(occupied, bias, blocks, inner, outer, col_count):
     halo = jax.ShapeDtypeStruct((8, 64, 128), jnp.bfloat16)
     return pl.pallas_call(
         main_kernel,
@@ -234,7 +248,7 @@
             jax.ShapeDtypeStruct((8, 128, 128), jnp.float32),
             halo,
             halo,
-            jax.ShapeDtypeStruct((col_count, 8, 128), jnp.float32),
+            jax.ShapeDtypeStruct((col_count, 1, 640), jnp.float32),
         ),
         in_specs=[SMEM_SPEC] + [VMEM_SPEC] * 4,
         out_specs=(VMEM_SPEC,) * 5,
@@ -248,13 +262,16 @@
             pltpu.VMEM((2048, 128), jnp.bfloat16),
             pltpu.VMEM((8, 256, 128), jnp.float32),
         ],
-        compiler_params=pltpu.CompilerParams(vmem_limit_bytes=40 << 20),
+        compiler_params=pltpu.CompilerParams(vmem_limit_bytes=24 << 20),
         name="attention_backward",
-    )(occupied, bias, blocks, left, right)
-
-
-def combine_kernel(dq_ref, own_ref, left_ref, right_ref, bias_ref, out_ref):
-    total = jnp.sum(bias_ref[...], axis=0)
+    )(occupied, bias, blocks, inner, outer)
+
+
+def combine_kernel(dq_ref, own_ref, inner_ref, outer_ref, bias_ref, out_ref):
+    even = (lax.axis_index("col") & 1) == 0
+    summed = jnp.sum(bias_ref[...], axis=0)
+    rows = [summed[:, 128 * k : 128 * k + 128] for k in range(5)]
+    total = jnp.concatenate(rows + [jnp.zeros((3, 128), jnp.float32)], axis=0)
     high = total.astype(jnp.bfloat16).astype(jnp.float32)
     rest = total - high
     middle = rest.astype(jnp.bfloat16).astype(jnp.float32)
@@ -262,24 +279,38 @@
     pieces = pieces.astype(jnp.bfloat16)
     for i in range(8):
         out_ref[i, 0:64] = dq_ref[i]
-        for at, ref in ((0, left_ref), (64, right_ref)):
-            summed = own_ref[i, at : at + 64] + ref[i].astype(jnp.float32)
+        inner, outer = inner_ref[i].astype(jnp.float32), outer_ref[i].astype(jnp.float32)
+        for at, share in (
+            (0, jnp.where(even, outer, inner)),
+            (64, jnp.where(even, inner, outer)),
+        ):
+            summed = own_ref[i, at : at + 64] + share
             out_ref[i, 64 + at : 128 + at] = summed.astype(jnp.bfloat16)
         out_ref[i, 192:224] = pieces
 
 
-def combine(dq, own, left, right, bias):
+def combine(dq, own, inner, outer, bias):
     return pl.pallas_call(
         combine_kernel,
         out_shape=jax.ShapeDtypeStruct((8, 224, 128), jnp.bfloat16),
         in_specs=[VMEM_SPEC] * 5,
         out_specs=VMEM_SPEC,
+        compiler_params=pltpu.CompilerParams(vmem_limit_bytes=8 << 20),
         name="combine",
-    )(dq, own, left, right, bias)
-
-
-def unpack_kernel(z_ref, gq_ref, gk_ref, gv_ref, gb_ref, bias_ref):
+    )(dq, own, inner, outer, bias)
+
+
+def unpack_kernel(z_ref, gq_hbm, gk_hbm, gv_hbm, gb_ref, gq_ref, gk_ref, gv_ref, bias_ref, sems):
     low = lanes_of((128, 128)) < 64
+    copies = [
+        pltpu.make_async_copy(source, target, sems.at[at])
+        for at, (source, target) in enumerate(
+            ((gq_ref, gq_hbm), (gk_ref, gk_hbm), (gv_ref, gv_hbm))
+        )
+    ]
+
+    def load(head, first, last):
+        return z_ref[head, first:last].astype(jnp.float32)
 
     def by_rows(block):
         split = block.reshape(2, 8, 8, 128)
@@ -287,21 +318,33 @@
 
     for pair in range(4):
         lanes = pl.ds(128 * pair, 128)
-        even = z_ref[2 * pair].astype(jnp.float32)
-        odd = z_ref[2 * pair + 1].astype(jnp.float32)
-        query = jnp.transpose(jnp.concatenate([even[0:64], odd[0:64]], axis=0))
-        gq_ref[:, :, lanes] = query.reshape(8, 16, 128).astype(jnp.bfloat16)
-        key = jnp.where(low, even[64:192], swap_halves(odd[64:192]))
-        value = jnp.where(low, swap_halves(even[64:192]), odd[64:192])
+        both = jnp.concatenate([load(2 * pair, 0, 64), load(2 * pair + 1, 0, 64)], axis=0)
+        gq_ref[:, :, lanes] = jnp.transpose(both).reshape(8, 16, 128).astype(jnp.bfloat16)
+    copies[0].start()
+    for pair in range(4):
+        lanes = pl.ds(128 * pair, 128)
+        key = jnp.where(
+            low, load(2 * pair, 64, 192), swap_halves(load(2 * pair + 1, 64, 192))
+        )
         gk_ref[:, :, lanes] = by_rows(key).astype(jnp.bfloat16)
+    copies[1].start()
+    for pair in range(4):
+        lanes = pl.ds(128 * pair, 128)
+        value = jnp.where(
+            low, swap_halves(load(2 * pair, 64, 192)), load(2 * pair + 1, 64, 192)
+        )
         gv_ref[:, :, lanes] = by_rows(value).astype(jnp.bfloat16)
-        for head, block in ((2 * pair, even), (2 * pair + 1, odd)):
-            bias_ref[head] = block[192:200] + block[200:208] + block[208:216]
+    copies[2].start()
+    for head in range(8):
+        pieces = load(head, 192, 224)
+        bias_ref[head] = pieces[0:8] + pieces[8:16] + pieces[16:24]
     for a in range(17):
         row = bias_ref[:, a // 4, :]
         if a % 4:
             row = pltpu.roll(row, 128 - 32 * (a % 4), 1)
         gb_ref[a] = row[:, 0:17]
+    for copy in copies:
+        copy.wait()
 
 
 def unpack(blocks):
@@ -310,28 +353,35 @@
         unpack_kernel,
         out_shape=(token, token, token, jax.ShapeDtypeStruct((17, 8, 17), jnp.float32)),
         in_specs=[VMEM_SPEC],
-        out_specs=(VMEM_SPEC,) * 4,
-        scratch_shapes=[pltpu.VMEM((8, 8, 128), jnp.float32)],
+        out_specs=(HBM_SPEC,) * 3 + (VMEM_SPEC,),
+        scratch_shapes=[pltpu.VMEM((8, 16, 512), jnp.bfloat16)] * 3
+        + [pltpu.VMEM((8, 8, 128), jnp.float32), pltpu.SemaphoreType.DMA((3,))],
+        compiler_params=pltpu.CompilerParams(vmem_limit_bytes=8 << 20),
         name="unpack",
     )(blocks)
 
 
 def shards(queries, keys, values, grad_out, rel_bias, occupied):
     col_count = lax.axis_size("col")
-    rightward = [(i, i + 1) for i in range(col_count - 1)]
-    leftward = [(i + 1, i) for i in range(col_count - 1)]
+    within = [(i, i ^ 1) for i in range(col_count)]
+    between = [(i, i - 1 if i % 2 == 0 else i + 1) for i in range(1, col_count - 1)]
+    odd = lax.axis_index("col") & 1
     packed = pack(queries, keys, values, grad_out)
     blocks = lax.all_to_all(packed, "row", 0, 0)
-    from_left = lax.ppermute(blocks[:, 192:256], "col", rightward)
-    from_right = lax.ppermute(blocks[:, 128:192], "col", leftward)
+    inner = lax.ppermute(
+        lax.dynamic_slice_in_dim(blocks, 192 - 64 * odd, 64, axis=1), "col", within
+    )
+    outer = lax.ppermute(
+        lax.dynamic_slice_in_dim(blocks, 128 + 64 * odd, 64, axis=1), "col", between
+    )
     bias = jnp.transpose(rel_bias, (1, 0, 2))
-    dq, own, out_left, out_right, bias_part = main(
-        occupied, bias, blocks, from_left, from_right, col_count
-    )
-    share_left = lax.ppermute(out_right, "col", rightward)
-    share_right = lax.ppermute(out_left, "col", leftward)
+    dq, own, out_inner, out_outer, bias_part = main(
+        occupied, bias, blocks, inner, outer, col_count
+    )
+    inner_share = lax.ppermute(out_inner, "col", within)
+    outer_share = lax.ppermute(out_outer, "col", between)
     bias_parts = lax.all_to_all(bias_part, "col", 0, 0)
-    returned = lax.all_to_all(combine(dq, own, share_left, share_right, bias_parts), "row", 0, 0)
+    returned = lax.all_to_all(combine(dq, own, inner_share, outer_share, bias_parts), "row", 0, 0)
     grad_query, grad_key, grad_value, grad_bias = unpack(returned)
     return grad_query, grad_key, grad_value, jnp.transpose(grad_bias, (1, 0, 2))
 

time: 76.5 us -> 65.7 us (0.86)
  blocking collectives: 32.6 us -> 11.7 us
  waiting for transfers between devices: 6.58 us -> 17.6 us
  starting transfers between devices: 23.6 us -> 26.7 us
  Pallas kernels: 10.3 us -> 8.06 us
  local copies, waits for them, and re-layouts: 2.16 us -> 0.03 us
    all_to_all x2 -> x1, blocking collectives: 32.6 us -> 11.7 us  [shards(): lax.all_to_all(combine(dq, own, inner_share, outer_share, bias_parts), 'r...]
    all_to_all x0 -> x1, waiting for transfers between devices: none -> 10.7 us  [shards(): blocks = lax.all_to_all(packed, 'row', 0, 0)]
    all_to_all x0 -> x1, starting transfers between devices: none -> 7.49 us  [shards(): blocks = lax.all_to_all(packed, 'row', 0, 0)]
    ppermute x4, starting transfers between devices: 12.8 us -> 9.15 us  [the longest x1 5.3 us: shards(): lax.ppermute(lax.dynamic_slice_in_dim(blocks, 128 + 64 * odd, 64, axis=1)...]
    unnamed x14 -> x4, local copies, waits for them, and re-layouts: 2.14 us -> 0.01 us
    pallas_call x1, Pallas kernels: 2 us -> 0.12 us  [combine(): pl.pallas_call(combine_kernel, out_shape=jax.ShapeDtypeStruct((8, 224, 12...]
    all_to_all x1, waiting for transfers between devices: 0.01 us -> 1.26 us  [shards(): bias_parts = lax.all_to_all(bias_part, 'col', 0, 0)]
    ppermute x4, waiting for transfers between devices: 6.58 us -> 5.67 us  [the longest x1 3.13 us: shards(): outer_share = lax.ppermute(out_outer, 'col', between)]
  transfers between devices with their start and end apart: 5 -> 6, of which waited for: 4 -> 4; matrix products, arithmetic and copies ran while one was open for 0% -> 0% of each run, Pallas kernels for 0% -> 0%
where the time goes in v3:
time: 65.7 us; the launch traced here: 64.8 us
  starting transfers between devices  26.7 us (41%)
  waiting for transfers between devices  17.6 us (27%)
  blocking collectives  11.7 us (18%)
  Pallas kernels  8.06 us (12%)
  between operations  0.7 us (1%)
    all_to_all x1, blocking collectives, shards(): lax.all_to_all(combine(dq, own, inner_share, outer_share, bias_parts), 'r...  11.7 us
    all_to_all x1, waiting for transfers between devices, shards(): blocks = lax.all_to_all(packed, 'row', 0, 0)  10.7 us
    all_to_all x1, starting transfers between devices, shards(): bias_parts = lax.all_to_all(bias_part, 'col', 0, 0)  10.1 us
    all_to_all x1, starting transfers between devices, shards(): blocks = lax.all_to_all(packed, 'row', 0, 0)  7.49 us
    ppermute x1, starting transfers between devices, shards(): lax.ppermute(lax.dynamic_slice_in_dim(blocks, 128 + 64 * odd, 64, axis=1)...  5.3 us
    pallas_call x1, Pallas kernels, main(): pl.pallas_call(main_kernel, out_shape=(halo, jax.ShapeDtypeStruct((8, 128...  4.28 us
    ppermute x1, starting transfers between devices, shards(): outer_share = lax.ppermute(out_outer, 'col', between)  3.44 us
    ppermute x1, waiting for transfers between devices, shards(): outer_share = lax.ppermute(out_outer, 'col', between)  3.13 us
  transfers between devices with their start and end apart: 6, of which 4 were waited for; matrix products, arithmetic and copies ran while one was open for 0% of the time, Pallas kernels for 0%

profile of v3, /device:TPU:1, one launch (start us, length us, event | category | flops | bytes accessed | tf_op | source)
XLA Modules:
  0.0 64.8 jit_solution(11046847223905588420)
XLA Ops:
  0.6 2.1 %pack.1 = bf16[8,256,128]{2,1,0:T(8,128)(2,1)} custom-call(bf16[8,16,512]{2,1,0:T(8,128)(2,1)} %q_hbm.1, bf16[8,16,512]{2,1,0:T(8,128)(2,1)} %k_hbm.1, bf16[8,16,512]{2,1,0:T(8,128)(2,1)} %v_hbm.1, bf16[8,16,512]{2,1,0:T(8,128)(2,1)} %g_hbm.1), custom_call_target="tpu_custom_call" | custom-call | tf_op jit(solution)/shard_map/pack/pallas_call | solution.py:61
  2.8 7.5 %all-to-all-start = ((bf16[8,256,128]{2,1,0:T(8,128)(2,1)}), bf16[8,256,128]{2,1,0:T(8,128)(2,1)S(1)}, u32[]{:S(2)}, u32[]{:S(2)}) async-start(bf16[8,256,128]{2,1,0:T(8,128)(2,1)} %pack.1), calls=%async_computation | async-start | bytes 1048576 | tf_op jit(solution)/shard_map/all_to_all | solution.py:370
  10.3 0.0 copy-start
  10.3 10.7 %all-to-all-done.x_ref = bf16[8,256,128]{2,1,0:T(8,128)(2,1)S(1)} async-done(((bf16[8,256,128]{2,1,0:T(8,128)(2,1)}), bf16[8,256,128]{2,1,0:T(8,128)(2,1)S(1)}, u32[]{:S(2)}, u32[]{:S(2)}) %all-to-all-start) | async-done | bytes 524320 | tf_op jit(solution)/shard_map/all_to_all | solution.py:370
  21.0 0.0 copy-start.1
  21.0 5.3 %collective-permute-start.1 = (bf16[8,64,128]{2,1,0:T(8,128)(2,1)S(1)}, bf16[8,64,128]{2,1,0:T(8,128)(2,1)S(1)}, u32[]{:S(2)}, u32[]{:S(2)}) collective-permute-start(bf16[8,64,128]{2,1,0:T(8,128)(2,1)S(1)} %get-tuple-element.22), channel_id=1, source_target_pairs={{1,2},{2,1},{3,4},{4,3},{5,6},{6,5},{7,8},{8,7},{9,10},{10,9},{11,... | collective-permute-start | bytes 393224 | tf_op jit(solution)/shard_map/ppermute | solution.py:374
  26.3 0.1 collective-permute-start
  26.4 2.5 %collective-permute-done.1.outer_ref = bf16[8,64,128]{2,1,0:T(8,128)(2,1)S(1)} collective-permute-done((bf16[8,64,128]{2,1,0:T(8,128)(2,1)S(1)}, bf16[8,64,128]{2,1,0:T(8,128)(2,1)S(1)}, u32[]{:S(2)}, u32[]{:S(2)}) %collective-permute-start.1) | collective-permute-done | bytes 131104 | tf_op jit(solution)/shard_map/ppermute | solution.py:374
  28.9 0.0 collective-permute-done.inner_ref
  28.9 0.0 copy-done
  28.9 0.0 copy-done.1
  28.9 4.3 %attention_backward.1 = (bf16[8,64,128]{2,1,0:T(8,128)(2,1)S(1)}, f32[8,128,128]{2,1,0:T(8,128)S(1)}, bf16[8,64,128]{2,1,0:T(8,128)(2,1)S(1)}, bf16[8,64,128]{2,1,0:T(8,128)(2,1)S(1)}, f32[32,1,640]{2,1,0:T(1,128)}) custom-call(s32[8,32]{1,0:T(8,128)S(1)} %copy-done.1, f32[17,8,17]{2,1,0:T(8,128)S(1)} %bitcast.2, ...), custom_call_target="tpu_custom_call" | custom-call | tf_op jit(solution)/shard_map/attention_backward/pallas_call | solution.py:244
  33.2 10.1 %all-to-all-start.1 = ((f32[32,1,640]{2,1,0:T(1,128)}), f32[32,1,640]{2,1,0:T(1,128)S(1)}, u32[]{:S(2)}, u32[]{:S(2)}) async-start(f32[32,1,640]{2,1,0:T(1,128)} %get-tuple-element.17), calls=%async_computation.1 | async-start | bytes 163840 | tf_op jit(solution)/shard_map/all_to_all | solution.py:383
  43.3 0.3 collective-permute-start.2
  43.6 3.4 %collective-permute-start.3 = (bf16[8,64,128]{2,1,0:T(8,128)(2,1)S(1)}, bf16[8,64,128]{2,1,0:T(8,128)(2,1)S(1)}, u32[]{:S(2)}, u32[]{:S(2)}) collective-permute-start(bf16[8,64,128]{2,1,0:T(8,128)(2,1)S(1)} %get-tuple-element.16), channel_id=1, source_target_pairs={{1,2},{2,1},{3,4},{4,3},{5,6},{6,5},{7,8},{8,7},{9,10},{10,9},{11,... | collective-permute-start | bytes 393224 | tf_op jit(solution)/shard_map/ppermute | solution.py:382
  47.1 0.0 collective-permute-done.2.inner_ref
  47.1 3.1 %collective-permute-done.3.outer_ref = bf16[8,64,128]{2,1,0:T(8,128)(2,1)S(1)} collective-permute-done((bf16[8,64,128]{2,1,0:T(8,128)(2,1)S(1)}, bf16[8,64,128]{2,1,0:T(8,128)(2,1)S(1)}, u32[]{:S(2)}, u32[]{:S(2)}) %collective-permute-start.3) | collective-permute-done | bytes 131104 | tf_op jit(solution)/shard_map/ppermute | solution.py:382
  50.2 1.3 %all-to-all-done.1.bias_ref = f32[32,1,640]{2,1,0:T(1,128)S(1)} async-done(((f32[32,1,640]{2,1,0:T(1,128)}), f32[32,1,640]{2,1,0:T(1,128)S(1)}, u32[]{:S(2)}, u32[]{:S(2)}) %all-to-all-start.1) | async-done | bytes 81952 | tf_op jit(solution)/shard_map/all_to_all | solution.py:383
  51.5 0.1 combine.1
  51.6 11.7 %all_to_all.15.z_ref = bf16[8,224,128]{2,1,0:T(8,128)(2,1)S(1)} all-to-all(bf16[8,224,128]{2,1,0:T(8,128)(2,1)S(1)} %combine.1), channel_id=1, replica_groups=mesh['row'=8,'col'=32] {'row'}, dimensions={0} | all-to-all | bytes 917504 | tf_op jit(solution)/shard_map/all_to_all | solution.py:384
  63.3 1.5 %unpack.1 = (bf16[8,16,512]{2,1,0:T(8,128)(2,1)}, bf16[8,16,512]{2,1,0:T(8,128)(2,1)}, bf16[8,16,512]{2,1,0:T(8,128)(2,1)}, f32[17,8,17]{2,1,0:T(8,128)}) custom-call(bf16[8,224,128]{2,1,0:T(8,128)(2,1)S(1)} %all_to_all.15.z_ref), custom_call_target="tpu_custom_call" | custom-call | tf_op jit(solution)/shard_map/unpack/pallas_call | solution.py:352
  (1 shorter events, 0.0 us)
Async XLA Ops:
  2.8 18.2 %all-to-all-start = ((bf16[8,256,128]{2,1,0:T(8,128)(2,1)}), bf16[8,256,128]{2,1,0:T(8,128)(2,1)S(1)}, u32[]{:S(2)}, u32[]{:S(2)}) async-start(bf16[8,256,128]{2,1,0:T(8,128)(2,1)} %pack.1), calls=%async_computation | async-start | bytes 1048576 | tf_op jit(solution)/shard_map/all_to_all | solution.py:370
  10.3 18.7 %copy-start = (f32[8,17,17]{2,0,1:T(8,128)S(1)}, f32[8,17,17]{2,0,1:T(8,128)}, u32[]{:S(2)}) copy-start(f32[8,17,17]{2,0,1:T(8,128)} %param.10) | copy-start | bytes 27748
  21.0 8.0 %copy-start.1 = (s32[8,32]{1,0:T(8,128)S(1)}, s32[8,32]{1,0:T(8,128)}, u32[]{:S(2)}) copy-start(s32[8,32]{1,0:T(8,128)} %occ_ref.1) | copy-start | bytes 3076
  21.0 7.9 %collective-permute-start.1 = (bf16[8,64,128]{2,1,0:T(8,128)(2,1)S(1)}, bf16[8,64,128]{2,1,0:T(8,128)(2,1)S(1)}, u32[]{:S(2)}, u32[]{:S(2)}) collective-permute-start(bf16[8,64,128]{2,1,0:T(8,128)(2,1)S(1)} %get-tuple-element.22), channel_id=1, source_target_pairs={{1,2},{2,1},{3,4},{4,3},{5,6},{6,5},{7,8},{8,7},{9,10},{10,9},{11,... | collective-permute-start | bytes 393224 | tf_op jit(solution)/shard_map/ppermute | solution.py:374
  26.3 2.6 %collective-permute-start = (bf16[8,64,128]{2,1,0:T(8,128)(2,1)S(1)}, bf16[8,64,128]{2,1,0:T(8,128)(2,1)S(1)}, u32[]{:S(2)}, u32[]{:S(2)}) collective-permute-start(bf16[8,64,128]{2,1,0:T(8,128)(2,1)S(1)} %get-tuple-element.23), channel_id=1, source_target_pairs={{0,1},{1,0},{2,3},{3,2},{4,5},{5,4},{6,7},{7,6},{8,9},{9,8},{10,11... | collective-permute-start | bytes 393224 | tf_op jit(solution)/shard_map/ppermute | solution.py:371
  33.2 18.3 %all-to-all-start.1 = ((f32[32,1,640]{2,1,0:T(1,128)}), f32[32,1,640]{2,1,0:T(1,128)S(1)}, u32[]{:S(2)}, u32[]{:S(2)}) async-start(f32[32,1,640]{2,1,0:T(1,128)} %get-tuple-element.17), calls=%async_computation.1 | async-start | bytes 163840 | tf_op jit(solution)/shard_map/all_to_all | solution.py:383
  43.3 3.8 %collective-permute-start.2 = (bf16[8,64,128]{2,1,0:T(8,128)(2,1)S(1)}, bf16[8,64,128]{2,1,0:T(8,128)(2,1)S(1)}, u32[]{:S(2)}, u32[]{:S(2)}) collective-permute-start(bf16[8,64,128]{2,1,0:T(8,128)(2,1)S(1)} %get-tuple-element.15), channel_id=1, source_target_pairs={{0,1},{1,0},{2,3},{3,2},{4,5},{5,4},{6,7},{7,6},{8,9},{9,8},{10,11... | collective-permute-start | bytes 393224 | tf_op jit(solution)/shard_map/ppermute | solution.py:381
  43.6 6.6 %collective-permute-start.3 = (bf16[8,64,128]{2,1,0:T(8,128)(2,1)S(1)}, bf16[8,64,128]{2,1,0:T(8,128)(2,1)S(1)}, u32[]{:S(2)}, u32[]{:S(2)}) collective-permute-start(bf16[8,64,128]{2,1,0:T(8,128)(2,1)S(1)} %get-tuple-element.16), channel_id=1, source_target_pairs={{1,2},{2,1},{3,4},{4,3},{5,6},{6,5},{7,8},{8,7},{9,10},{10,9},{11,... | collective-permute-start | bytes 393224 | tf_op jit(solution)/shard_map/ppermute | solution.py:382

commit v4 on v3

--- a/solution.py
+++ b/solution.py
@@ -11,7 +11,6 @@
 MASKED = -1e30
 VMEM_SPEC = pl.BlockSpec(memory_space=pltpu.VMEM)
 HBM_SPEC = pl.BlockSpec(memory_space=pltpu.HBM)
-SMEM_SPEC = pl.BlockSpec(memory_space=pltpu.SMEM)
 
 
 def lanes_of(shape):
@@ -22,39 +21,49 @@
     return pltpu.roll(array, 64, 1)
 
 
-def pack_kernel(q_hbm, k_hbm, v_hbm, g_hbm, out_ref, q_ref, k_ref, v_ref, g_ref, sems):
+def pack_kernel(
+    q_hbm, k_hbm, v_hbm, g_hbm, out_hbm, q_ref, k_ref, v_ref, g_ref, out_ref, in_sems, out_sems
+):
     copies = [
-        pltpu.make_async_copy(source, target, sems.at[at])
+        pltpu.make_async_copy(source, target, in_sems.at[at])
         for at, (source, target) in enumerate(
             ((q_hbm, q_ref), (g_hbm, g_ref), (k_hbm, k_ref), (v_hbm, v_ref))
         )
     ]
     for copy in copies:
         copy.start()
-    for copy in copies:
+    low = lanes_of((128, 128)) < 64
+
+    def load(ref, pair):
+        return ref[:, :, 128 * pair : 128 * pair + 128].astype(jnp.float32)
+
+    def by_halves(block):
+        split = block.reshape(8, 2, 8, 128)
+        return jnp.concatenate([split[:, half].reshape(64, 128) for half in range(2)], axis=0)
+
+    def store(pair, at, first, second):
+        even = jnp.where(low, first, swap_halves(second))
+        odd = jnp.where(low, swap_halves(first), second)
+        out_ref[2 * pair, at : at + 128, :] = even.astype(jnp.bfloat16)
+        out_ref[2 * pair + 1, at : at + 128, :] = odd.astype(jnp.bfloat16)
+
+    copies[0].wait()
+    copies[1].wait()
+    for pair in range(4):
+        query = load(q_ref, pair).reshape(128, 128) * 0.125
+        store(pair, 0, query, load(g_ref, pair).reshape(128, 128))
+    copies[2].wait()
+    copies[3].wait()
+    returns = []
+    for pair in range(4):
+        store(pair, 128, by_halves(load(k_ref, pair)), by_halves(load(v_ref, pair)))
+        heads = pl.ds(2 * pair, 2)
+        returns.append(
+            pltpu.make_async_copy(out_ref.at[heads], out_hbm.at[heads], out_sems.at[pair])
+        )
+        returns[-1].start()
+    for copy in returns:
         copy.wait()
-    low = lanes_of((128, 128)) < 64
-    for pair in range(4):
-        lanes = pl.ds(128 * pair, 128)
-
-        def load(ref):
-            return ref[:, :, lanes].astype(jnp.float32)
-
-        def by_halves(block):
-            split = block.reshape(8, 2, 8, 128)
-            return jnp.concatenate(
-                [split[:, half].reshape(64, 128) for half in range(2)], axis=0
-            )
-
-        query = load(q_ref).reshape(128, 128) * 0.125
-        grad = load(g_ref).reshape(128, 128)
-        key = by_halves(load(k_ref))
-        value = by_halves(load(v_ref))
-        for at, first, second in ((0, query, grad), (128, key, value)):
-            even = jnp.where(low, first, swap_halves(second))
-            odd = jnp.where(low, swap_halves(first), second)
-            out_ref[2 * pair, at : at + 128, :] = even.astype(jnp.bfloat16)
-            out_ref[2 * pair + 1, at : at + 128, :] = odd.astype(jnp.bfloat16)
 
 
 def pack(queries, keys, values, grad_out):
@@ -62,9 +71,13 @@
         pack_kernel,
         out_shape=jax.ShapeDtypeStruct((8, 256, 128), jnp.bfloat16),
         in_specs=[HBM_SPEC] * 4,
-        out_specs=VMEM_SPEC,
+        out_specs=HBM_SPEC,
         scratch_shapes=[pltpu.VMEM((8, 16, 512), jnp.bfloat16)] * 4
-        + [pltpu.SemaphoreType.DMA((4,))],
+        + [
+            pltpu.VMEM((8, 256, 128), jnp.bfloat16),
+            pltpu.SemaphoreType.DMA((4,)),
+            pltpu.SemaphoreType.DMA((4,)),
+        ],
         compiler_params=pltpu.CompilerParams(vmem_limit_bytes=60 << 20),
         name="pack",
     )(queries, keys, values, grad_out)
@@ -142,20 +155,24 @@
 ):
     head = lax.axis_index("row")
     col = lax.axis_index("col")
-    col_count = occ_ref.shape[1]
     even = (col & 1) == 0
     build_table(head, bias_ref, rows_ref, table_ref)
     low = lanes_of((128, 128)) < 64
     sums_ref[...] = jnp.zeros_like(sums_ref)
 
-    def filled(row, at):
-        inside = (at >= 0) & (at < col_count)
-        return inside & (occ_ref[row, jnp.clip(at, 0, col_count - 1)] > 0)
-
-    def penalty(row, at):
-        return jnp.where(filled(row, at), jnp.float32(0.0), jnp.float32(MASKED))
-
-    marks = []
+    lane = lanes_of(occ_ref.shape)
+
+    def filled(at):
+        column = jnp.sum(jnp.where(lane == at, occ_ref[...], 0), axis=1, keepdims=True)
+        return jnp.broadcast_to(column, (8, 128)) > 0
+
+    own_filled = filled(col)
+    used = jnp.where(own_filled, 1.0, 0.0)
+    own_mark = jnp.where(own_filled, 0.0, MASKED)
+    left_mark = jnp.where(filled(col - 1), 0.0, MASKED)
+    right_mark = jnp.where(filled(col + 1), 0.0, MASKED)
+    chunk_marks = (left_mark, own_mark, own_mark, right_mark)
+
     for j in range(8):
         inner, outer = inner_ref[j], outer_ref[j]
         kv_ref[256 * j : 256 * j + 64] = jnp.where(even, outer, inner)
@@ -167,8 +184,6 @@
         zero = jnp.zeros_like(query_grad)
         qg_ref[256 * j : 256 * j + 128] = jnp.where(low, query_grad, zero)
         qg_ref[256 * j + 128 : 256 * j + 256] = jnp.where(low, zero, query_grad)
-        own = penalty(j, col)
-        marks.append((penalty(j, col - 1), own, own, penalty(j, col + 1)))
 
     def window(i):
         steps = [step for step in range(3) if 0 <= i - 1 + step < 8]
@@ -190,7 +205,9 @@
         for step in steps:
             for chunk in range(4):
                 at = 256 * (step - steps[0]) + 64 * chunk
-                bias = table_ref[step, chunk].reshape(64, 128) + marks[i - 1 + step][chunk]
+                row = i - 1 + step
+                mark = chunk_marks[chunk][row : row + 1]
+                bias = table_ref[step, chunk].reshape(64, 128) + mark
                 shifted.append(scores[at : at + 64] * LOG2E + bias)
         shifted = jnp.concatenate(shifted, axis=0)
         top = jnp.max(shifted, axis=0, keepdims=True)
@@ -199,8 +216,7 @@
         weighted = jnp.sum(exponent * grads, axis=0, keepdims=True)
         inverse = 1.0 / total
         delta = weighted * inverse
-        used = jnp.where(filled(i, col), jnp.float32(1.0), jnp.float32(0.0))
-        weights = exponent * (inverse * used)
+        weights = exponent * (inverse * used[i : i + 1])
         grad_scores = weights * (grads - delta)
         sums_ref[steps[0] : steps[-1] + 1] += grad_scores.reshape(count, 4, 8, 8, 128)
         return weights.astype(jnp.bfloat16), grad_scores.astype(jnp.bfloat16)
@@ -250,7 +266,7 @@
             halo,
             jax.ShapeDtypeStruct((col_count, 1, 640), jnp.float32),
         ),
-        in_specs=[SMEM_SPEC] + [VMEM_SPEC] * 4,
+        in_specs=[VMEM_SPEC] * 5,
         out_specs=(VMEM_SPEC,) * 5,
         scratch_shapes=[
             pltpu.VMEM((24, 128), jnp.float32),
@@ -270,13 +286,16 @@
 def combine_kernel(dq_ref, own_ref, inner_ref, outer_ref, bias_ref, out_ref):
     even = (lax.axis_index("col") & 1) == 0
     summed = jnp.sum(bias_ref[...], axis=0)
-    rows = [summed[:, 128 * k : 128 * k + 128] for k in range(5)]
-    total = jnp.concatenate(rows + [jnp.zeros((3, 128), jnp.float32)], axis=0)
-    high = total.astype(jnp.bfloat16).astype(jnp.float32)
-    rest = total - high
+    high = summed.astype(jnp.bfloat16).astype(jnp.float32)
+    rest = summed - high
     middle = rest.astype(jnp.bfloat16).astype(jnp.float32)
-    pieces = jnp.concatenate([high, middle, rest - middle, jnp.zeros_like(total)], axis=0)
-    pieces = pieces.astype(jnp.bfloat16)
+    rows = [
+        piece[:, 128 * k : 128 * k + 128]
+        for piece in (high, middle, rest - middle)
+        for k in range(5)
+    ]
+    rows.append(jnp.zeros((1, 128), jnp.float32))
+    pieces = jnp.concatenate(rows, axis=0).astype(jnp.bfloat16)
     for i in range(8):
         out_ref[i, 0:64] = dq_ref[i]
         inner, outer = inner_ref[i].astype(jnp.float32), outer_ref[i].astype(jnp.float32)
@@ -286,13 +305,13 @@
         ):
             summed = own_ref[i, at : at + 64] + share
             out_ref[i, 64 + at : 128 + at] = summed.astype(jnp.bfloat16)
-        out_ref[i, 192:224] = pieces
+        out_ref[i, 192:208] = pieces
 
 
 def combine(dq, own, inner, outer, bias):
     return pl.pallas_call(
         combine_kernel,
-        out_shape=jax.ShapeDtypeStruct((8, 224, 128), jnp.bfloat16),
+        out_shape=jax.ShapeDtypeStruct((8, 208, 128), jnp.bfloat16),
         in_specs=[VMEM_SPEC] * 5,
         out_specs=VMEM_SPEC,
         compiler_params=pltpu.CompilerParams(vmem_limit_bytes=8 << 20),
@@ -300,7 +319,7 @@
     )(dq, own, inner, outer, bias)
 
 
-def unpack_kernel(z_ref, gq_hbm, gk_hbm, gv_hbm, gb_ref, gq_ref, gk_ref, gv_ref, bias_ref, sems):
+def unpack_kernel(z_ref, gq_hbm, gk_hbm, gv_hbm, gb_ref, gq_ref, gk_ref, gv_ref, pieces_ref, sems):
     low = lanes_of((128, 128)) < 64
     copies = [
         pltpu.make_async_copy(source, target, sems.at[at])
@@ -336,10 +355,10 @@
         gv_ref[:, :, lanes] = by_rows(value).astype(jnp.bfloat16)
     copies[2].start()
     for head in range(8):
-        pieces = load(head, 192, 224)
-        bias_ref[head] = pieces[0:8] + pieces[8:16] + pieces[16:24]
+        pieces_ref[head] = load(head, 192, 208)
     for a in range(17):
-        row = bias_ref[:, a // 4, :]
+        k = a // 4
+        row = pieces_ref[:, k, :] + pieces_ref[:, k + 5, :] + pieces_ref[:, k + 10, :]
         if a % 4:
             row = pltpu.roll(row, 128 - 32 * (a % 4), 1)
         gb_ref[a] = row[:, 0:17]
@@ -355,7 +374,7 @@
         in_specs=[VMEM_SPEC],
         out_specs=(HBM_SPEC,) * 3 + (VMEM_SPEC,),
         scratch_shapes=[pltpu.VMEM((8, 16, 512), jnp.bfloat16)] * 3
-        + [pltpu.VMEM((8, 8, 128), jnp.float32), pltpu.SemaphoreType.DMA((3,))],
+        + [pltpu.VMEM((8, 16, 128), jnp.float32), pltpu.SemaphoreType.DMA((3,))],
         compiler_params=pltpu.CompilerParams(vmem_limit_bytes=8 << 20),
         name="unpack",
     )(blocks)
@@ -378,8 +397,8 @@
     dq, own, out_inner, out_outer, bias_part = main(
         occupied, bias, blocks, inner, outer, col_count
     )
+    outer_share = lax.ppermute(out_outer, "col", between)
     inner_share = lax.ppermute(out_inner, "col", within)
-    outer_share = lax.ppermute(out_outer, "col", between)
     bias_parts = lax.all_to_all(bias_part, "col", 0, 0)
     returned = lax.all_to_all(combine(dq, own, inner_share, outer_share, bias_parts), "row", 0, 0)
     grad_query, grad_key, grad_value, grad_bias = unpack(returned)

time: 65.7 us -> 64.8 us (0.986)
  no operation moved by 1% of the time
where the time goes in v4:
time: 64.8 us; the launch traced here: 64 us
  starting transfers between devices  26.7 us (41%)
  waiting for transfers between devices  17.6 us (27%)
  blocking collectives  11.5 us (18%)
  Pallas kernels  7.43 us (11%)
  between operations  0.71 us (1%)
    all_to_all x1, blocking collectives, shards(): lax.all_to_all(combine(dq, own, inner_share, outer_share, bias_parts), 'r...  11.5 us
    all_to_all x1, waiting for transfers between devices, shards(): blocks = lax.all_to_all(packed, 'row', 0, 0)  10.7 us
    all_to_all x1, starting transfers between devices, shards(): bias_parts = lax.all_to_all(bias_part, 'col', 0, 0)  10.1 us
    all_to_all x1, starting transfers between devices, shards(): blocks = lax.all_to_all(packed, 'row', 0, 0)  7.49 us
    ppermute x1, starting transfers between devices, shards(): lax.ppermute(lax.dynamic_slice_in_dim(blocks, 128 + 64 * odd, 64, axis=1)...  5.3 us
    pallas_call x1, Pallas kernels, main(): pl.pallas_call(main_kernel, out_shape=(halo, jax.ShapeDtypeStruct((8, 128...  3.71 us
    ppermute x1, starting transfers between devices, shards(): outer_share = lax.ppermute(out_outer, 'col', between)  3.44 us
    ppermute x1, waiting for transfers between devices, shards(): outer_share = lax.ppermute(out_outer, 'col', between)  3.13 us
  transfers between devices with their start and end apart: 6, of which 4 were waited for; matrix products, arithmetic and copies ran while one was open for 0% of the time, Pallas kernels for 0%

profile of v4, /device:TPU:1, one launch (start us, length us, event | category | flops | bytes accessed | tf_op | source)
XLA Modules:
  0.0 64.0 jit_solution(14502722868986117344)
XLA Ops:
  0.6 2.1 %pack.1 = bf16[8,256,128]{2,1,0:T(8,128)(2,1)} custom-call(bf16[8,16,512]{2,1,0:T(8,128)(2,1)} %q_hbm.1, bf16[8,16,512]{2,1,0:T(8,128)(2,1)} %k_hbm.1, bf16[8,16,512]{2,1,0:T(8,128)(2,1)} %v_hbm.1, bf16[8,16,512]{2,1,0:T(8,128)(2,1)} %g_hbm.1), custom_call_target="tpu_custom_call" | custom-call | tf_op jit(solution)/shard_map/pack/pallas_call | solution.py:70
  2.7 7.5 %all-to-all-start = ((bf16[8,256,128]{2,1,0:T(8,128)(2,1)}), bf16[8,256,128]{2,1,0:T(8,128)(2,1)S(1)}, u32[]{:S(2)}, u32[]{:S(2)}) async-start(bf16[8,256,128]{2,1,0:T(8,128)(2,1)} %pack.1), calls=%async_computation | async-start | bytes 1048576 | tf_op jit(solution)/shard_map/all_to_all | solution.py:389
  10.2 0.0 copy-start
  10.2 10.7 %all-to-all-done.x_ref = bf16[8,256,128]{2,1,0:T(8,128)(2,1)S(1)} async-done(((bf16[8,256,128]{2,1,0:T(8,128)(2,1)}), bf16[8,256,128]{2,1,0:T(8,128)(2,1)S(1)}, u32[]{:S(2)}, u32[]{:S(2)}) %all-to-all-start) | async-done | bytes 524320 | tf_op jit(solution)/shard_map/all_to_all | solution.py:389
  20.9 0.0 copy-start.1
  20.9 5.3 %collective-permute-start.1 = (bf16[8,64,128]{2,1,0:T(8,128)(2,1)S(1)}, bf16[8,64,128]{2,1,0:T(8,128)(2,1)S(1)}, u32[]{:S(2)}, u32[]{:S(2)}) collective-permute-start(bf16[8,64,128]{2,1,0:T(8,128)(2,1)S(1)} %get-tuple-element.22), channel_id=1, source_target_pairs={{1,2},{2,1},{3,4},{4,3},{5,6},{6,5},{7,8},{8,7},{9,10},{10,9},{11,... | collective-permute-start | bytes 393224 | tf_op jit(solution)/shard_map/ppermute | solution.py:393
  26.2 0.1 collective-permute-start
  26.3 2.5 %collective-permute-done.1.outer_ref = bf16[8,64,128]{2,1,0:T(8,128)(2,1)S(1)} collective-permute-done((bf16[8,64,128]{2,1,0:T(8,128)(2,1)S(1)}, bf16[8,64,128]{2,1,0:T(8,128)(2,1)S(1)}, u32[]{:S(2)}, u32[]{:S(2)}) %collective-permute-start.1) | collective-permute-done | bytes 131104 | tf_op jit(solution)/shard_map/ppermute | solution.py:393
  28.9 0.0 collective-permute-done.inner_ref
  28.9 0.0 copy-done
  28.9 0.0 copy-done.1
  28.9 3.7 %attention_backward.1 = (bf16[8,64,128]{2,1,0:T(8,128)(2,1)S(1)}, f32[8,128,128]{2,1,0:T(8,128)S(1)}, bf16[8,64,128]{2,1,0:T(8,128)(2,1)S(1)}, bf16[8,64,128]{2,1,0:T(8,128)(2,1)S(1)}, f32[32,1,640]{2,1,0:T(1,128)}) custom-call(s32[8,32]{1,0:T(8,128)S(1)} %copy-done.1, f32[17,8,17]{2,1,0:T(8,128)S(1)} %bitcast.2, ...), custom_call_target="tpu_custom_call" | custom-call | tf_op jit(solution)/shard_map/attention_backward/pallas_call | solution.py:260
  32.6 10.1 %all-to-all-start.1 = ((f32[32,1,640]{2,1,0:T(1,128)}), f32[32,1,640]{2,1,0:T(1,128)S(1)}, u32[]{:S(2)}, u32[]{:S(2)}) async-start(f32[32,1,640]{2,1,0:T(1,128)} %get-tuple-element.17), calls=%async_computation.1 | async-start | bytes 163840 | tf_op jit(solution)/shard_map/all_to_all | solution.py:402
  42.7 0.3 collective-permute-start.2
  43.0 3.4 %collective-permute-start.3 = (bf16[8,64,128]{2,1,0:T(8,128)(2,1)S(1)}, bf16[8,64,128]{2,1,0:T(8,128)(2,1)S(1)}, u32[]{:S(2)}, u32[]{:S(2)}) collective-permute-start(bf16[8,64,128]{2,1,0:T(8,128)(2,1)S(1)} %get-tuple-element.16), channel_id=1, source_target_pairs={{1,2},{2,1},{3,4},{4,3},{5,6},{6,5},{7,8},{8,7},{9,10},{10,9},{11,... | collective-permute-start | bytes 393224 | tf_op jit(solution)/shard_map/ppermute | solution.py:400
  46.4 0.0 collective-permute-done.2.inner_ref
  46.4 3.1 %collective-permute-done.3.outer_ref = bf16[8,64,128]{2,1,0:T(8,128)(2,1)S(1)} collective-permute-done((bf16[8,64,128]{2,1,0:T(8,128)(2,1)S(1)}, bf16[8,64,128]{2,1,0:T(8,128)(2,1)S(1)}, u32[]{:S(2)}, u32[]{:S(2)}) %collective-permute-start.3) | collective-permute-done | bytes 131104 | tf_op jit(solution)/shard_map/ppermute | solution.py:400
  49.6 1.3 %all-to-all-done.1.bias_ref = f32[32,1,640]{2,1,0:T(1,128)S(1)} async-done(((f32[32,1,640]{2,1,0:T(1,128)}), f32[32,1,640]{2,1,0:T(1,128)S(1)}, u32[]{:S(2)}, u32[]{:S(2)}) %all-to-all-start.1) | async-done | bytes 81952 | tf_op jit(solution)/shard_map/all_to_all | solution.py:402
  50.8 0.1 combine.1
  51.0 11.5 %all_to_all.15.z_ref = bf16[8,208,128]{2,1,0:T(8,128)(2,1)S(1)} all-to-all(bf16[8,208,128]{2,1,0:T(8,128)(2,1)S(1)} %combine.1), channel_id=1, replica_groups=mesh['row'=8,'col'=32] {'row'}, dimensions={0} | all-to-all | bytes 851968 | tf_op jit(solution)/shard_map/all_to_all | solution.py:403
  62.5 1.5 %unpack.1 = (bf16[8,16,512]{2,1,0:T(8,128)(2,1)}, bf16[8,16,512]{2,1,0:T(8,128)(2,1)}, bf16[8,16,512]{2,1,0:T(8,128)(2,1)}, f32[17,8,17]{2,1,0:T(8,128)}) custom-call(bf16[8,208,128]{2,1,0:T(8,128)(2,1)S(1)} %all_to_all.15.z_ref), custom_call_target="tpu_custom_call" | custom-call | tf_op jit(solution)/shard_map/unpack/pallas_call | solution.py:371
  (1 shorter events, 0.0 us)
Async XLA Ops:
  2.7 18.2 %all-to-all-start = ((bf16[8,256,128]{2,1,0:T(8,128)(2,1)}), bf16[8,256,128]{2,1,0:T(8,128)(2,1)S(1)}, u32[]{:S(2)}, u32[]{:S(2)}) async-start(bf16[8,256,128]{2,1,0:T(8,128)(2,1)} %pack.1), calls=%async_computation | async-start | bytes 1048576 | tf_op jit(solution)/shard_map/all_to_all | solution.py:389
  10.2 18.7 %copy-start = (f32[8,17,17]{2,0,1:T(8,128)S(1)}, f32[8,17,17]{2,0,1:T(8,128)}, u32[]{:S(2)}) copy-start(f32[8,17,17]{2,0,1:T(8,128)} %param.10) | copy-start | bytes 27748
  20.9 8.0 %copy-start.1 = (s32[8,32]{1,0:T(8,128)S(1)}, s32[8,32]{1,0:T(8,128)}, u32[]{:S(2)}) copy-start(s32[8,32]{1,0:T(8,128)} %occ_ref.1) | copy-start | bytes 3076
  20.9 7.9 %collective-permute-start.1 = (bf16[8,64,128]{2,1,0:T(8,128)(2,1)S(1)}, bf16[8,64,128]{2,1,0:T(8,128)(2,1)S(1)}, u32[]{:S(2)}, u32[]{:S(2)}) collective-permute-start(bf16[8,64,128]{2,1,0:T(8,128)(2,1)S(1)} %get-tuple-element.22), channel_id=1, source_target_pairs={{1,2},{2,1},{3,4},{4,3},{5,6},{6,5},{7,8},{8,7},{9,10},{10,9},{11,... | collective-permute-start | bytes 393224 | tf_op jit(solution)/shard_map/ppermute | solution.py:393
  26.2 2.6 %collective-permute-start = (bf16[8,64,128]{2,1,0:T(8,128)(2,1)S(1)}, bf16[8,64,128]{2,1,0:T(8,128)(2,1)S(1)}, u32[]{:S(2)}, u32[]{:S(2)}) collective-permute-start(bf16[8,64,128]{2,1,0:T(8,128)(2,1)S(1)} %get-tuple-element.23), channel_id=1, source_target_pairs={{0,1},{1,0},{2,3},{3,2},{4,5},{5,4},{6,7},{7,6},{8,9},{9,8},{10,11... | collective-permute-start | bytes 393224 | tf_op jit(solution)/shard_map/ppermute | solution.py:390
  32.6 18.3 %all-to-all-start.1 = ((f32[32,1,640]{2,1,0:T(1,128)}), f32[32,1,640]{2,1,0:T(1,128)S(1)}, u32[]{:S(2)}, u32[]{:S(2)}) async-start(f32[32,1,640]{2,1,0:T(1,128)} %get-tuple-element.17), calls=%async_computation.1 | async-start | bytes 163840 | tf_op jit(solution)/shard_map/all_to_all | solution.py:402
  42.7 3.8 %collective-permute-start.2 = (bf16[8,64,128]{2,1,0:T(8,128)(2,1)S(1)}, bf16[8,64,128]{2,1,0:T(8,128)(2,1)S(1)}, u32[]{:S(2)}, u32[]{:S(2)}) collective-permute-start(bf16[8,64,128]{2,1,0:T(8,128)(2,1)S(1)} %get-tuple-element.15), channel_id=1, source_target_pairs={{0,1},{1,0},{2,3},{3,2},{4,5},{5,4},{6,7},{7,6},{8,9},{9,8},{10,11... | collective-permute-start | bytes 393224 | tf_op jit(solution)/shard_map/ppermute | solution.py:401
  43.0 6.6 %collective-permute-start.3 = (bf16[8,64,128]{2,1,0:T(8,128)(2,1)S(1)}, bf16[8,64,128]{2,1,0:T(8,128)(2,1)S(1)}, u32[]{:S(2)}, u32[]{:S(2)}) collective-permute-start(bf16[8,64,128]{2,1,0:T(8,128)(2,1)S(1)} %get-tuple-element.16), channel_id=1, source_target_pairs={{1,2},{2,1},{3,4},{4,3},{5,6},{6,5},{7,8},{8,7},{9,10},{10,9},{11,... | collective-permute-start | bytes 393224 | tf_op jit(solution)/shard_map/ppermute | solution.py:400

commit v5 on v4

--- a/solution.py
+++ b/solution.py
@@ -21,11 +21,13 @@
     return pltpu.roll(array, 64, 1)
 
 
-def pack_kernel(
-    q_hbm, k_hbm, v_hbm, g_hbm, out_hbm, q_ref, k_ref, v_ref, g_ref, out_ref, in_sems, out_sems
-):
+def even_col():
+    return (lax.axis_index("col") & 1) == 0
+
+
+def pack_kernel(q_hbm, k_hbm, v_hbm, g_hbm, out_ref, q_ref, k_ref, v_ref, g_ref, sems):
     copies = [
-        pltpu.make_async_copy(source, target, in_sems.at[at])
+        pltpu.make_async_copy(source, target, sems.at[at])
         for at, (source, target) in enumerate(
             ((q_hbm, q_ref), (g_hbm, g_ref), (k_hbm, k_ref), (v_hbm, v_ref))
         )
@@ -33,13 +35,17 @@
     for copy in copies:
         copy.start()
     low = lanes_of((128, 128)) < 64
+    even_col_here = even_col()
 
     def load(ref, pair):
         return ref[:, :, 128 * pair : 128 * pair + 128].astype(jnp.float32)
 
     def by_halves(block):
         split = block.reshape(8, 2, 8, 128)
-        return jnp.concatenate([split[:, half].reshape(64, 128) for half in range(2)], axis=0)
+        left, right = split[:, 0].reshape(64, 128), split[:, 1].reshape(64, 128)
+        inner = jnp.where(even_col_here, right, left)
+        outer = jnp.where(even_col_here, left, right)
+        return jnp.concatenate([inner, outer], axis=0)
 
     def store(pair, at, first, second):
         even = jnp.where(low, first, swap_halves(second))
@@ -54,16 +60,8 @@
         store(pair, 0, query, load(g_ref, pair).reshape(128, 128))
     copies[2].wait()
     copies[3].wait()
-    returns = []
     for pair in range(4):
         store(pair, 128, by_halves(load(k_ref, pair)), by_halves(load(v_ref, pair)))
-        heads = pl.ds(2 * pair, 2)
-        returns.append(
-            pltpu.make_async_copy(out_ref.at[heads], out_hbm.at[heads], out_sems.at[pair])
-        )
-        returns[-1].start()
-    for copy in returns:
-        copy.wait()
 
 
 def pack(queries, keys, values, grad_out):
@@ -71,16 +69,21 @@
         pack_kernel,
         out_shape=jax.ShapeDtypeStruct((8, 256, 128), jnp.bfloat16),
         in_specs=[HBM_SPEC] * 4,
-        out_specs=HBM_SPEC,
+        out_specs=VMEM_SPEC,
         scratch_shapes=[pltpu.VMEM((8, 16, 512), jnp.bfloat16)] * 4
-        + [
-            pltpu.VMEM((8, 256, 128), jnp.bfloat16),
-            pltpu.SemaphoreType.DMA((4,)),
-            pltpu.SemaphoreType.DMA((4,)),
-        ],
-        compiler_params=pltpu.CompilerParams(vmem_limit_bytes=60 << 20),
+        + [pltpu.SemaphoreType.DMA((4,))],
+        compiler_params=pltpu.CompilerParams(vmem_limit_bytes=8 << 20),
         name="pack",
-    )(queries, keys, values, grad_out)
+    )(
+        *(
+            pltpu.with_memory_space_constraint(array, pltpu.HBM)
+            for array in (queries, keys, values, grad_out)
+        )
+    )
+
+
+def chunk_place(chunk):
+    return jnp.where(even_col(), 3 - chunk, chunk)
 
 
 def build_table(head, bias_ref, rows_ref, table_ref):
@@ -107,13 +110,13 @@
         table = jnp.where(query_row == row, padded[7 - row : 31 - row], table)
     table = table.reshape(3, 8, 4, 8, 128)
     for chunk in range(4):
-        table_ref[:, chunk] = table[:, :, chunk]
+        table_ref[:, chunk_place(chunk)] = table[:, :, chunk]
 
 
 def contract_bias(sums_ref, skew_ref, bias_out_ref):
     query_row = lanes_of((17, 8, 128)) >> 4
     for chunk in range(4):
-        by_row = sums_ref[:, chunk].reshape(24, 8, 128)
+        by_row = sums_ref[:, chunk_place(chunk)].reshape(24, 8, 128)
         picked = by_row[0:17]
         for row in range(1, 8):
             picked = jnp.where(query_row == row, by_row[row : row + 17], picked)
@@ -155,7 +158,7 @@
 ):
     head = lax.axis_index("row")
     col = lax.axis_index("col")
-    even = (col & 1) == 0
+    even = even_col()
     build_table(head, bias_ref, rows_ref, table_ref)
     low = lanes_of((128, 128)) < 64
     sums_ref[...] = jnp.zeros_like(sums_ref)
@@ -169,15 +172,14 @@
     own_filled = filled(col)
     used = jnp.where(own_filled, 1.0, 0.0)
     own_mark = jnp.where(own_filled, 0.0, MASKED)
-    left_mark = jnp.where(filled(col - 1), 0.0, MASKED)
-    right_mark = jnp.where(filled(col + 1), 0.0, MASKED)
-    chunk_marks = (left_mark, own_mark, own_mark, right_mark)
+    inner_mark = jnp.where(filled(jnp.where(even, col + 1, col - 1)), 0.0, MASKED)
+    outer_mark = jnp.where(filled(jnp.where(even, col - 1, col + 1)), 0.0, MASKED)
+    chunk_marks = (inner_mark, own_mark, own_mark, outer_mark)
 
     for j in range(8):
-        inner, outer = inner_ref[j], outer_ref[j]
-        kv_ref[256 * j : 256 * j + 64] = jnp.where(even, outer, inner)
+        kv_ref[256 * j : 256 * j + 64] = inner_ref[j]
         kv_ref[256 * j + 64 : 256 * j + 192] = x_ref[j, 128:256]
-        kv_ref[256 * j + 192 : 256 * j + 256] = jnp.where(even, inner, outer)
+        kv_ref[256 * j + 192 : 256 * j + 256] = outer_ref[j]
         flipped = jnp.transpose(kv_ref[256 * j : 256 * j + 256])
         kt_ref[:, 256 * j : 256 * j + 256] = flipped[0:64]
         query_grad = x_ref[j, 0:128]
@@ -241,10 +243,9 @@
             if not (step == 2 or i == 0):
                 part = part + p_ref[j]
             if step == 0 or i == 7:
-                left, right = part[0:64], part[192:256]
-                out_inner_ref[j] = jnp.where(even, right, left).astype(jnp.bfloat16)
+                out_inner_ref[j] = part[0:64].astype(jnp.bfloat16)
                 own_ref[j] = part[64:192]
-                out_outer_ref[j] = jnp.where(even, left, right).astype(jnp.bfloat16)
+                out_outer_ref[j] = part[192:256].astype(jnp.bfloat16)
             else:
                 p_ref[j] = part
 
@@ -284,7 +285,6 @@
 
 
 def combine_kernel(dq_ref, own_ref, inner_ref, outer_ref, bias_ref, out_ref):
-    even = (lax.axis_index("col") & 1) == 0
     summed = jnp.sum(bias_ref[...], axis=0)
     high = summed.astype(jnp.bfloat16).astype(jnp.float32)
     rest = summed - high
@@ -298,12 +298,8 @@
     pieces = jnp.concatenate(rows, axis=0).astype(jnp.bfloat16)
     for i in range(8):
         out_ref[i, 0:64] = dq_ref[i]
-        inner, outer = inner_ref[i].astype(jnp.float32), outer_ref[i].astype(jnp.float32)
-        for at, share in (
-            (0, jnp.where(even, outer, inner)),
-            (64, jnp.where(even, inner, outer)),
-        ):
-            summed = own_ref[i, at : at + 64] + share
+        for at, ref in ((0, inner_ref), (64, outer_ref)):
+            summed = own_ref[i, at : at + 64] + ref[i].astype(jnp.float32)
             out_ref[i, 64 + at : 128 + at] = summed.astype(jnp.bfloat16)
         out_ref[i, 192:208] = pieces
 
@@ -320,6 +316,7 @@
 
 
 def unpack_kernel(z_ref, gq_hbm, gk_hbm, gv_hbm, gb_ref, gq_ref, gk_ref, gv_ref, pieces_ref, sems):
+    even_col_here = even_col()
     low = lanes_of((128, 128)) < 64
     copies = [
         pltpu.make_async_copy(source, target, sems.at[at])
@@ -332,8 +329,10 @@
         return z_ref[head, first:last].astype(jnp.float32)
 
     def by_rows(block):
-        split = block.reshape(2, 8, 8, 128)
-        return jnp.concatenate([split[0], split[1]], axis=1)
+        inner, outer = block[0:64].reshape(8, 8, 128), block[64:128].reshape(8, 8, 128)
+        left = jnp.where(even_col_here, outer, inner)
+        right = jnp.where(even_col_here, inner, outer)
+        return jnp.concatenate([left, right], axis=1)
 
     for pair in range(4):
         lanes = pl.ds(128 * pair, 128)
@@ -384,15 +383,10 @@
     col_count = lax.axis_size("col")
     within = [(i, i ^ 1) for i in range(col_count)]
     between = [(i, i - 1 if i % 2 == 0 else i + 1) for i in range(1, col_count - 1)]
-    odd = lax.axis_index("col") & 1
     packed = pack(queries, keys, values, grad_out)
     blocks = lax.all_to_all(packed, "row", 0, 0)
-    inner = lax.ppermute(
-        lax.dynamic_slice_in_dim(blocks, 192 - 64 * odd, 64, axis=1), "col", within
-    )
-    outer = lax.ppermute(
-        lax.dynamic_slice_in_dim(blocks, 128 + 64 * odd, 64, axis=1), "col", between
-    )
+    inner = lax.ppermute(blocks[:, 128:192], "col", within)
+    outer = lax.ppermute(blocks[:, 192:256], "col", between)
     bias = jnp.transpose(rel_bias, (1, 0, 2))
     dq, own, out_inner, out_outer, bias_part = main(
         occupied, bias, blocks, inner, outer, col_count

time: 64.8 us -> 64.1 us (0.989)
  blocking collectives: 11.5 us -> 29.5 us
  waiting for transfers between devices: 17.6 us -> 6.93 us
  starting transfers between devices: 26.7 us -> 19.4 us
  Pallas kernels: 7.43 us -> 6.74 us
    all_to_all x0 -> x1, blocking collectives: none -> 18 us  [shards(): blocks = lax.all_to_all(packed, 'row', 0, 0)]
    all_to_all x1 -> x0, waiting for transfers between devices: 10.7 us -> none  [shards(): blocks = lax.all_to_all(packed, 'row', 0, 0)]
    all_to_all x1 -> x0, starting transfers between devices: 7.49 us -> none  [shards(): blocks = lax.all_to_all(packed, 'row', 0, 0)]
    pallas_call x1, Pallas kernels: 2.07 us -> 1.28 us  [pack(): pl.pallas_call(pack_kernel, out_shape=jax.ShapeDtypeStruct((8, 256, 128),...]
  transfers between devices with their start and end apart: 6 -> 5, of which waited for: 4 -> 3; matrix products, arithmetic and copies ran while one was open for 0% -> 0% of each run, Pallas kernels for 0% -> 0%
where the time goes in v5:
time: 64.1 us; the launch traced here: 63.3 us
  blocking collectives  29.5 us (46%)
  starting transfers between devices  19.4 us (30%)
  waiting for transfers between devices  6.93 us (11%)
  Pallas kernels  6.74 us (11%)
  between operations  0.7 us (1%)
    all_to_all x1, blocking collectives, shards(): blocks = lax.all_to_all(packed, 'row', 0, 0)  18 us
    all_to_all x1, blocking collectives, shards(): lax.all_to_all(combine(dq, own, inner_share, outer_share, bias_parts), 'r...  11.6 us
    all_to_all x1, starting transfers between devices, shards(): bias_parts = lax.all_to_all(bias_part, 'col', 0, 0)  10.1 us
    ppermute x1, starting transfers between devices, shards(): outer = lax.ppermute(blocks[:, 192:256], 'col', between)  5.43 us
    pallas_call x1, Pallas kernels, main(): pl.pallas_call(main_kernel, out_shape=(halo, jax.ShapeDtypeStruct((8, 128...  3.83 us
    ppermute x1, starting transfers between devices, shards(): outer_share = lax.ppermute(out_outer, 'col', between)  3.44 us
    ppermute x1, waiting for transfers between devices, shards(): outer_share = lax.ppermute(out_outer, 'col', between)  3.13 us
    ppermute x1, waiting for transfers between devices, shards(): outer = lax.ppermute(blocks[:, 192:256], 'col', between)  2.54 us
  transfers between devices with their start and end apart: 5, of which 3 were waited for; matrix products, arithmetic and copies ran while one was open for 0% of the time, Pallas kernels for 0%

profile of v5, /device:TPU:1, one launch (start us, length us, event | category | flops | bytes accessed | tf_op | source)
XLA Modules:
  0.0 63.3 jit_solution(5395621971921540532)
XLA Ops:
  0.6 1.3 %pack.1 = bf16[8,256,128]{2,1,0:T(8,128)(2,1)S(1)} custom-call(bf16[8,16,512]{2,1,0:T(8,128)(2,1)} %q_hbm.1, bf16[8,16,512]{2,1,0:T(8,128)(2,1)} %k_hbm.1, bf16[8,16,512]{2,1,0:T(8,128)(2,1)} %v_hbm.1, bf16[8,16,512]{2,1,0:T(8,128)(2,1)} %g_hbm.1), custom_call_target="tpu_custom_call" | custom-call | tf_op jit(solution)/shard_map/pack/pallas_call | solution.py:68
  1.9 18.0 %all_to_all.15.x_ref = bf16[8,256,128]{2,1,0:T(8,128)(2,1)S(1)} all-to-all(bf16[8,256,128]{2,1,0:T(8,128)(2,1)S(1)} %pack.1), channel_id=1, replica_groups=mesh['row'=8,'col'=32] {'row'}, dimensions={0} | all-to-all | bytes 1048576 | tf_op jit(solution)/shard_map/all_to_all | solution.py:387
  19.9 0.0 copy-start
  19.9 0.0 copy-start.1
  19.9 5.4 %collective-permute-start.1 = (bf16[8,64,128]{2,1,0:T(8,128)(2,1)S(1)}, bf16[8,64,128]{2,1,0:T(8,128)(2,1)S(1)}, u32[]{:S(2)}, u32[]{:S(2)}) collective-permute-start(bf16[8,64,128]{2,1,0:T(8,128)(2,1)S(1)} %get-tuple-element.22), channel_id=1, source_target_pairs={{1,2},{2,1},{3,4},{4,3},{5,6},{6,5},{7,8},{8,7},{9,10},{10,9},{11,... | collective-permute-start | bytes 393224 | tf_op jit(solution)/shard_map/ppermute | solution.py:389
  25.3 0.1 collective-permute-start
  25.4 2.5 %collective-permute-done.1.outer_ref = bf16[8,64,128]{2,1,0:T(8,128)(2,1)S(1)} collective-permute-done((bf16[8,64,128]{2,1,0:T(8,128)(2,1)S(1)}, bf16[8,64,128]{2,1,0:T(8,128)(2,1)S(1)}, u32[]{:S(2)}, u32[]{:S(2)}) %collective-permute-start.1) | collective-permute-done | bytes 131104 | tf_op jit(solution)/shard_map/ppermute | solution.py:389
  28.0 0.0 collective-permute-done.inner_ref
  28.0 0.0 copy-done
  28.0 0.0 copy-done.1
  28.0 3.8 %attention_backward.1 = (bf16[8,64,128]{2,1,0:T(8,128)(2,1)S(1)}, f32[8,128,128]{2,1,0:T(8,128)S(1)}, bf16[8,64,128]{2,1,0:T(8,128)(2,1)S(1)}, bf16[8,64,128]{2,1,0:T(8,128)(2,1)S(1)}, f32[32,1,640]{2,1,0:T(1,128)}) custom-call(s32[8,32]{1,0:T(8,128)S(1)} %copy-done.1, f32[17,8,17]{2,1,0:T(8,128)S(1)} %bitcast.2, bf16[8,256,128]{2,1,0:T(8,128)(2,1)S(1)} %all_to_all.15.x_ref, ...), custom_call_target="tpu_custom_call" | custom-call | tf_op jit(solution)/shard_map/attention_backward/pallas_call | solution.py:261
  31.8 10.1 %all-to-all-start.1 = ((f32[32,1,640]{2,1,0:T(1,128)}), f32[32,1,640]{2,1,0:T(1,128)S(1)}, u32[]{:S(2)}, u32[]{:S(2)}) async-start(f32[32,1,640]{2,1,0:T(1,128)} %get-tuple-element.17), calls=%async_computation.1 | async-start | bytes 163840 | tf_op jit(solution)/shard_map/all_to_all | solution.py:396
  41.9 0.3 collective-permute-start.2
  42.2 3.4 %collective-permute-start.3 = (bf16[8,64,128]{2,1,0:T(8,128)(2,1)S(1)}, bf16[8,64,128]{2,1,0:T(8,128)(2,1)S(1)}, u32[]{:S(2)}, u32[]{:S(2)}) collective-permute-start(bf16[8,64,128]{2,1,0:T(8,128)(2,1)S(1)} %get-tuple-element.16), channel_id=1, source_target_pairs={{1,2},{2,1},{3,4},{4,3},{5,6},{6,5},{7,8},{8,7},{9,10},{10,9},{11,... | collective-permute-start | bytes 393224 | tf_op jit(solution)/shard_map/ppermute | solution.py:394
  45.7 0.0 collective-permute-done.2.inner_ref
  45.7 3.1 %collective-permute-done.3.outer_ref = bf16[8,64,128]{2,1,0:T(8,128)(2,1)S(1)} collective-permute-done((bf16[8,64,128]{2,1,0:T(8,128)(2,1)S(1)}, bf16[8,64,128]{2,1,0:T(8,128)(2,1)S(1)}, u32[]{:S(2)}, u32[]{:S(2)}) %collective-permute-start.3) | collective-permute-done | bytes 131104 | tf_op jit(solution)/shard_map/ppermute | solution.py:394
  48.8 1.3 %all-to-all-done.1.bias_ref = f32[32,1,640]{2,1,0:T(1,128)S(1)} async-done(((f32[32,1,640]{2,1,0:T(1,128)}), f32[32,1,640]{2,1,0:T(1,128)S(1)}, u32[]{:S(2)}, u32[]{:S(2)}) %all-to-all-start.1) | async-done | bytes 81952 | tf_op jit(solution)/shard_map/all_to_all | solution.py:396
  50.1 0.1 combine.1
  50.2 11.6 %all_to_all.16.z_ref = bf16[8,208,128]{2,1,0:T(8,128)(2,1)S(1)} all-to-all(bf16[8,208,128]{2,1,0:T(8,128)(2,1)S(1)} %combine.1), channel_id=1, replica_groups=mesh['row'=8,'col'=32] {'row'}, dimensions={0} | all-to-all | bytes 851968 | tf_op jit(solution)/shard_map/all_to_all | solution.py:397
  61.8 1.5 %unpack.1 = (bf16[8,16,512]{2,1,0:T(8,128)(2,1)}, bf16[8,16,512]{2,1,0:T(8,128)(2,1)}, bf16[8,16,512]{2,1,0:T(8,128)(2,1)}, f32[17,8,17]{2,1,0:T(8,128)}) custom-call(bf16[8,208,128]{2,1,0:T(8,128)(2,1)S(1)} %all_to_all.16.z_ref), custom_call_target="tpu_custom_call" | custom-call | tf_op jit(solution)/shard_map/unpack/pallas_call | solution.py:370
  (1 shorter events, 0.0 us)
Async XLA Ops:
  19.9 8.1 %copy-start = (f32[8,17,17]{2,0,1:T(8,128)S(1)}, f32[8,17,17]{2,0,1:T(8,128)}, u32[]{:S(2)}) copy-start(f32[8,17,17]{2,0,1:T(8,128)} %param.10) | copy-start | bytes 27748
  19.9 8.1 %copy-start.1 = (s32[8,32]{1,0:T(8,128)S(1)}, s32[8,32]{1,0:T(8,128)}, u32[]{:S(2)}) copy-start(s32[8,32]{1,0:T(8,128)} %occ_ref.1) | copy-start | bytes 3076
  19.9 8.1 %collective-permute-start.1 = (bf16[8,64,128]{2,1,0:T(8,128)(2,1)S(1)}, bf16[8,64,128]{2,1,0:T(8,128)(2,1)S(1)}, u32[]{:S(2)}, u32[]{:S(2)}) collective-permute-start(bf16[8,64,128]{2,1,0:T(8,128)(2,1)S(1)} %get-tuple-element.22), channel_id=1, source_target_pairs={{1,2},{2,1},{3,4},{4,3},{5,6},{6,5},{7,8},{8,7},{9,10},{10,9},{11,... | collective-permute-start | bytes 393224 | tf_op jit(solution)/shard_map/ppermute | solution.py:389
  25.3 2.6 %collective-permute-start = (bf16[8,64,128]{2,1,0:T(8,128)(2,1)S(1)}, bf16[8,64,128]{2,1,0:T(8,128)(2,1)S(1)}, u32[]{:S(2)}, u32[]{:S(2)}) collective-permute-start(bf16[8,64,128]{2,1,0:T(8,128)(2,1)S(1)} %get-tuple-element.23), channel_id=1, source_target_pairs={{0,1},{1,0},{2,3},{3,2},{4,5},{5,4},{6,7},{7,6},{8,9},{9,8},{10,11... | collective-permute-start | bytes 393224 | tf_op jit(solution)/shard_map/ppermute | solution.py:388
  31.8 18.3 %all-to-all-start.1 = ((f32[32,1,640]{2,1,0:T(1,128)}), f32[32,1,640]{2,1,0:T(1,128)S(1)}, u32[]{:S(2)}, u32[]{:S(2)}) async-start(f32[32,1,640]{2,1,0:T(1,128)} %get-tuple-element.17), calls=%async_computation.1 | async-start | bytes 163840 | tf_op jit(solution)/shard_map/all_to_all | solution.py:396
  41.9 3.8 %collective-permute-start.2 = (bf16[8,64,128]{2,1,0:T(8,128)(2,1)S(1)}, bf16[8,64,128]{2,1,0:T(8,128)(2,1)S(1)}, u32[]{:S(2)}, u32[]{:S(2)}) collective-permute-start(bf16[8,64,128]{2,1,0:T(8,128)(2,1)S(1)} %get-tuple-element.15), channel_id=1, source_target_pairs={{0,1},{1,0},{2,3},{3,2},{4,5},{5,4},{6,7},{7,6},{8,9},{9,8},{10,11... | collective-permute-start | bytes 393224 | tf_op jit(solution)/shard_map/ppermute | solution.py:395
  42.2 6.6 %collective-permute-start.3 = (bf16[8,64,128]{2,1,0:T(8,128)(2,1)S(1)}, bf16[8,64,128]{2,1,0:T(8,128)(2,1)S(1)}, u32[]{:S(2)}, u32[]{:S(2)}) collective-permute-start(bf16[8,64,128]{2,1,0:T(8,128)(2,1)S(1)} %get-tuple-element.16), channel_id=1, source_target_pairs={{1,2},{2,1},{3,4},{4,3},{5,6},{6,5},{7,8},{8,7},{9,10},{10,9},{11,... | collective-permute-start | bytes 393224 | tf_op jit(solution)/shard_map/ppermute | solution.py:394

commit v6 on v5

--- a/solution.py
+++ b/solution.py
@@ -136,9 +136,53 @@
     bias_out_ref[...] = jnp.broadcast_to(total[0:1, :][None], bias_out_ref.shape)
 
 
+def window(i):
+    steps = [step for step in range(3) if 0 <= i - 1 + step < 8]
+    return steps, i - 1 + steps[0], len(steps)
+
+
+def against(keys, queries):
+    return lax.dot_general(
+        keys, queries, (((1,), (1,)), ((), ())), preferred_element_type=jnp.float32
+    )
+
+
+def own_kernel(bias_ref, x_ref, table_ref, qg_ref, scores_ref, rows_ref):
+    low = lanes_of((128, 128)) < 64
+    for j in range(8):
+        query_grad = x_ref[j, 0:128]
+        zero = jnp.zeros_like(query_grad)
+        qg_ref[256 * j : 256 * j + 128] = jnp.where(low, query_grad, zero)
+        qg_ref[256 * j + 128 : 256 * j + 256] = jnp.where(low, zero, query_grad)
+    for i in range(8):
+        steps, first, count = window(i)
+        keys = x_ref[first : first + count, 128:256].reshape(128 * count, 128)
+        at = 128 * steps[0]
+        scores_ref[i, at : at + 128 * count] = against(keys, qg_ref[256 * i : 256 * i + 256])
+    build_table(lax.axis_index("row"), bias_ref, rows_ref, table_ref)
+
+
+def own_scores(bias, blocks):
+    return pl.pallas_call(
+        own_kernel,
+        out_shape=(
+            jax.ShapeDtypeStruct((3, 4, 8, 8, 128), jnp.float32),
+            jax.ShapeDtypeStruct((2048, 128), jnp.bfloat16),
+            jax.ShapeDtypeStruct((8, 384, 256), jnp.float32),
+        ),
+        in_specs=[VMEM_SPEC] * 2,
+        out_specs=(VMEM_SPEC,) * 3,
+        scratch_shapes=[pltpu.VMEM((24, 128), jnp.float32)],
+        compiler_params=pltpu.CompilerParams(vmem_limit_bytes=8 << 20),
+        name="own_scores",
+    )(bias, blocks)
+
+
 def main_kernel(
     occ_ref,
-    bias_ref,
+    table_ref,
+    qg_ref,
+    scores_ref,
     x_ref,
     inner_ref,
     outer_ref,
@@ -147,20 +191,14 @@
     out_inner_ref,
     out_outer_ref,
     bias_out_ref,
-    rows_ref,
-    table_ref,
     sums_ref,
     skew_ref,
     kv_ref,
     kt_ref,
-    qg_ref,
     p_ref,
 ):
-    head = lax.axis_index("row")
     col = lax.axis_index("col")
     even = even_col()
-    build_table(head, bias_ref, rows_ref, table_ref)
-    low = lanes_of((128, 128)) < 64
     sums_ref[...] = jnp.zeros_like(sums_ref)
 
     lane = lanes_of(occ_ref.shape)
@@ -182,36 +220,35 @@
         kv_ref[256 * j + 192 : 256 * j + 256] = outer_ref[j]
         flipped = jnp.transpose(kv_ref[256 * j : 256 * j + 256])
         kt_ref[:, 256 * j : 256 * j + 256] = flipped[0:64]
-        query_grad = x_ref[j, 0:128]
-        zero = jnp.zeros_like(query_grad)
-        qg_ref[256 * j : 256 * j + 128] = jnp.where(low, query_grad, zero)
-        qg_ref[256 * j + 128 : 256 * j + 256] = jnp.where(low, zero, query_grad)
-
-    def window(i):
-        steps = [step for step in range(3) if 0 <= i - 1 + step < 8]
-        return steps, i - 1 + steps[0], len(steps)
 
     def products(i):
         _, first, count = window(i)
-        return lax.dot_general(
-            kv_ref[256 * first : 256 * (first + count)],
-            qg_ref[256 * i : 256 * i + 256],
-            (((1,), (1,)), ((), ())),
-            preferred_element_type=jnp.float32,
-        )
+        return [
+            against(
+                ref[first : first + count].reshape(64 * count, 128),
+                qg_ref[256 * i : 256 * i + 256],
+            )
+            for ref in (inner_ref, outer_ref)
+        ]
 
     def softmax(i, both):
         steps, first, count = window(i)
-        scores, grads = both[:, 0:128], both[:, 128:256]
-        shifted = []
+        shifted, grads = [], []
         for step in steps:
+            halo = 64 * (step - steps[0])
+            parts = (
+                both[0][halo : halo + 64],
+                scores_ref[i, 128 * step : 128 * step + 64],
+                scores_ref[i, 128 * step + 64 : 128 * step + 128],
+                both[1][halo : halo + 64],
+            )
             for chunk in range(4):
-                at = 256 * (step - steps[0]) + 64 * chunk
                 row = i - 1 + step
                 mark = chunk_marks[chunk][row : row + 1]
                 bias = table_ref[step, chunk].reshape(64, 128) + mark
-                shifted.append(scores[at : at + 64] * LOG2E + bias)
-        shifted = jnp.concatenate(shifted, axis=0)
+                shifted.append(parts[chunk][:, 0:128] * LOG2E + bias)
+                grads.append(parts[chunk][:, 128:256])
+        shifted, grads = jnp.concatenate(shifted, axis=0), jnp.concatenate(grads, axis=0)
         top = jnp.max(shifted, axis=0, keepdims=True)
         exponent = jnp.exp2(shifted - top)
         total = jnp.sum(exponent, axis=0, keepdims=True)
@@ -256,7 +293,7 @@
     contract_bias(sums_ref, skew_ref, bias_out_ref)
 
 
-def main(occupied, bias, blocks, inner, outer, col_count):
+def main(occupied, table, qg, scores, blocks, inner, outer, col_count):
     halo = jax.ShapeDtypeStruct((8, 64, 128), jnp.bfloat16)
     return pl.pallas_call(
         main_kernel,
@@ -267,21 +304,18 @@
             halo,
             jax.ShapeDtypeStruct((col_count, 1, 640), jnp.float32),
         ),
-        in_specs=[VMEM_SPEC] * 5,
+        in_specs=[VMEM_SPEC] * 7,
         out_specs=(VMEM_SPEC,) * 5,
         scratch_shapes=[
-            pltpu.VMEM((24, 128), jnp.float32),
-            pltpu.VMEM((3, 4, 8, 8, 128), jnp.float32),
             pltpu.VMEM((3, 4, 8, 8, 128), jnp.float32),
             pltpu.VMEM((17, 4, 8, 128), jnp.float32),
             pltpu.VMEM((2048, 128), jnp.bfloat16),
             pltpu.VMEM((64, 2048), jnp.bfloat16),
-            pltpu.VMEM((2048, 128), jnp.bfloat16),
             pltpu.VMEM((8, 256, 128), jnp.float32),
         ],
         compiler_params=pltpu.CompilerParams(vmem_limit_bytes=24 << 20),
         name="attention_backward",
-    )(occupied, bias, blocks, inner, outer)
+    )(occupied, table, qg, scores, blocks, inner, outer)
 
 
 def combine_kernel(dq_ref, own_ref, inner_ref, outer_ref, bias_ref, out_ref):
@@ -389,7 +423,7 @@
     outer = lax.ppermute(blocks[:, 192:256], "col", between)
     bias = jnp.transpose(rel_bias, (1, 0, 2))
     dq, own, out_inner, out_outer, bias_part = main(
-        occupied, bias, blocks, inner, outer, col_count
+        occupied, *own_scores(bias, blocks), blocks, inner, outer, col_count
     )
     outer_share = lax.ppermute(out_outer, "col", between)
     inner_share = lax.ppermute(out_inner, "col", within)

time: 64.1 us -> 63.6 us (level)
  waiting for transfers between devices: 6.93 us -> 5.43 us
  local copies, waits for them, and re-layouts: 0.03 us -> 0.9 us
    ppermute x1, waiting for transfers between devices: 2.54 us -> 1.03 us  [shards(): outer = lax.ppermute(blocks[:, 192:256], 'col', between)]
    unnamed x4, local copies, waits for them, and re-layouts: 0.01 us -> 0.88 us
  transfers between devices with their start and end apart: 5 -> 5, of which waited for: 3 -> 3; matrix products, arithmetic and copies ran while one was open for 0% -> 0% of each run, Pallas kernels for 0% -> 1%
where the time goes in v6:
time: 63.6 us; the launch traced here: 62.8 us
  blocking collectives  29.5 us (46%)
  starting transfers between devices  19.2 us (30%)
  Pallas kernels  7 us (11%)
  waiting for transfers between devices  5.43 us (9%)
  local copies, waits for them, and re-layouts  0.9 us (1%)
  between operations  0.72 us (1%)
    all_to_all x1, blocking collectives, shards(): blocks = lax.all_to_all(packed, 'row', 0, 0)  18 us
    all_to_all x1, blocking collectives, shards(): lax.all_to_all(combine(dq, own, inner_share, outer_share, bias_parts), 'r...  11.6 us
    all_to_all x1, starting transfers between devices, shards(): bias_parts = lax.all_to_all(bias_part, 'col', 0, 0)  10.1 us
    ppermute x1, starting transfers between devices, shards(): outer = lax.ppermute(blocks[:, 192:256], 'col', between)  5.3 us
    pallas_call x1, Pallas kernels, main(): pl.pallas_call(main_kernel, out_shape=(halo, jax.ShapeDtypeStruct((8, 128...  3.46 us
    ppermute x1, starting transfers between devices, shards(): outer_share = lax.ppermute(out_outer, 'col', between)  3.44 us
    ppermute x1, waiting for transfers between devices, shards(): outer_share = lax.ppermute(out_outer, 'col', between)  3.13 us
    pallas_call x1, Pallas kernels, unpack(): pl.pallas_call(unpack_kernel, out_shape=(token, token, token, jax.ShapeDt...  1.52 us
  transfers between devices with their start and end apart: 5, of which 3 were waited for; matrix products, arithmetic and copies ran while one was open for 0% of the time, Pallas kernels for 1%

profile of v6, /device:TPU:1, one launch (start us, length us, event | category | flops | bytes accessed | tf_op | source)
XLA Modules:
  0.0 62.8 jit_solution(10293057041287601781)
XLA Ops:
  0.6 0.0 copy-start.1
  0.6 1.3 %pack.1 = bf16[8,256,128]{2,1,0:T(8,128)(2,1)S(1)} custom-call(bf16[8,16,512]{2,1,0:T(8,128)(2,1)} %q_hbm.1, bf16[8,16,512]{2,1,0:T(8,128)(2,1)} %k_hbm.1, bf16[8,16,512]{2,1,0:T(8,128)(2,1)} %v_hbm.1, bf16[8,16,512]{2,1,0:T(8,128)(2,1)} %g_hbm.1), custom_call_target="tpu_custom_call" | custom-call | tf_op jit(solution)/shard_map/pack/pallas_call | solution.py:68
  1.9 18.0 %all_to_all.15.x_ref = bf16[8,256,128]{2,1,0:T(8,128)(2,1)S(1)} all-to-all(bf16[8,256,128]{2,1,0:T(8,128)(2,1)S(1)} %pack.1), channel_id=1, replica_groups=mesh['row'=8,'col'=32] {'row'}, dimensions={0} | all-to-all | bytes 1048576 | tf_op jit(solution)/shard_map/all_to_all | solution.py:421
  19.9 5.3 %collective-permute-start.1 = (bf16[8,64,128]{2,1,0:T(8,128)(2,1)S(1)}, bf16[8,64,128]{2,1,0:T(8,128)(2,1)S(1)}, u32[]{:S(2)}, u32[]{:S(2)}) collective-permute-start(bf16[8,64,128]{2,1,0:T(8,128)(2,1)S(1)} %get-tuple-element.28), channel_id=1, source_target_pairs={{1,2},{2,1},{3,4},{4,3},{5,6},{6,5},{7,8},{8,7},{9,10},{10,9},{11,... | collective-permute-start | bytes 393224 | tf_op jit(solution)/shard_map/ppermute | solution.py:423
  25.2 0.1 collective-permute-start
  25.3 0.0 copy-start
  25.3 0.9 %copy-done = f32[8,17,17]{2,0,1:T(8,128)S(1)} copy-done((f32[8,17,17]{2,0,1:T(8,128)S(1)}, f32[8,17,17]{2,0,1:T(8,128)}, u32[]{:S(2)}) %copy-start) | copy-done | bytes 9272
  26.2 0.6 own_scores.1
  26.8 1.0 %collective-permute-done.1.outer_ref = bf16[8,64,128]{2,1,0:T(8,128)(2,1)S(1)} collective-permute-done((bf16[8,64,128]{2,1,0:T(8,128)(2,1)S(1)}, bf16[8,64,128]{2,1,0:T(8,128)(2,1)S(1)}, u32[]{:S(2)}, u32[]{:S(2)}) %collective-permute-start.1) | collective-permute-done | bytes 131104 | tf_op jit(solution)/shard_map/ppermute | solution.py:423
  27.9 0.0 collective-permute-done.inner_ref
  27.9 0.0 copy-done.1
  27.9 3.5 %attention_backward.1 = (bf16[8,64,128]{2,1,0:T(8,128)(2,1)S(1)}, f32[8,128,128]{2,1,0:T(8,128)S(1)}, bf16[8,64,128]{2,1,0:T(8,128)(2,1)S(1)}, bf16[8,64,128]{2,1,0:T(8,128)(2,1)S(1)}, f32[32,1,640]{2,1,0:T(1,128)}) custom-call(s32[8,32]{1,0:T(8,128)S(1)} %copy-done.1, f32[3,4,8,8,128]{4,3,2,1,0:T(8,128)S(1)} %get-tuple-element.16.table_ref, ...), custom_call_target="tpu_custom_call" | custom-call | tf_op jit(solution)/shard_map/attention_backward/pallas_call | solution.py:298
  31.3 10.1 %all-to-all-start.1 = ((f32[32,1,640]{2,1,0:T(1,128)}), f32[32,1,640]{2,1,0:T(1,128)S(1)}, u32[]{:S(2)}, u32[]{:S(2)}) async-start(f32[32,1,640]{2,1,0:T(1,128)} %get-tuple-element.23), calls=%async_computation.1 | async-start | bytes 163840 | tf_op jit(solution)/shard_map/all_to_all | solution.py:430
  41.4 0.3 collective-permute-start.2
  41.7 3.4 %collective-permute-start.3 = (bf16[8,64,128]{2,1,0:T(8,128)(2,1)S(1)}, bf16[8,64,128]{2,1,0:T(8,128)(2,1)S(1)}, u32[]{:S(2)}, u32[]{:S(2)}) collective-permute-start(bf16[8,64,128]{2,1,0:T(8,128)(2,1)S(1)} %get-tuple-element.22), channel_id=1, source_target_pairs={{1,2},{2,1},{3,4},{4,3},{5,6},{6,5},{7,8},{8,7},{9,10},{10,9},{11,... | collective-permute-start | bytes 393224 | tf_op jit(solution)/shard_map/ppermute | solution.py:428
  45.2 0.0 collective-permute-done.2.inner_ref
  45.2 3.1 %collective-permute-done.3.outer_ref = bf16[8,64,128]{2,1,0:T(8,128)(2,1)S(1)} collective-permute-done((bf16[8,64,128]{2,1,0:T(8,128)(2,1)S(1)}, bf16[8,64,128]{2,1,0:T(8,128)(2,1)S(1)}, u32[]{:S(2)}, u32[]{:S(2)}) %collective-permute-start.3) | collective-permute-done | bytes 131104 | tf_op jit(solution)/shard_map/ppermute | solution.py:428
  48.3 1.3 %all-to-all-done.1.bias_ref = f32[32,1,640]{2,1,0:T(1,128)S(1)} async-done(((f32[32,1,640]{2,1,0:T(1,128)}), f32[32,1,640]{2,1,0:T(1,128)S(1)}, u32[]{:S(2)}, u32[]{:S(2)}) %all-to-all-start.1) | async-done | bytes 81952 | tf_op jit(solution)/shard_map/all_to_all | solution.py:430
  49.6 0.1 combine.1
  49.7 11.6 %all_to_all.16.z_ref = bf16[8,208,128]{2,1,0:T(8,128)(2,1)S(1)} all-to-all(bf16[8,208,128]{2,1,0:T(8,128)(2,1)S(1)} %combine.1), channel_id=1, replica_groups=mesh['row'=8,'col'=32] {'row'}, dimensions={0} | all-to-all | bytes 851968 | tf_op jit(solution)/shard_map/all_to_all | solution.py:431
  61.3 1.5 %unpack.1 = (bf16[8,16,512]{2,1,0:T(8,128)(2,1)}, bf16[8,16,512]{2,1,0:T(8,128)(2,1)}, bf16[8,16,512]{2,1,0:T(8,128)(2,1)}, f32[17,8,17]{2,1,0:T(8,128)}) custom-call(bf16[8,208,128]{2,1,0:T(8,128)(2,1)S(1)} %all_to_all.16.z_ref), custom_call_target="tpu_custom_call" | custom-call | tf_op jit(solution)/shard_map/unpack/pallas_call | solution.py:404
  (1 shorter events, 0.0 us)
Async XLA Ops:
  0.6 27.2 %copy-start.1 = (s32[8,32]{1,0:T(8,128)S(1)}, s32[8,32]{1,0:T(8,128)}, u32[]{:S(2)}) copy-start(s32[8,32]{1,0:T(8,128)} %occ_ref.1) | copy-start | bytes 3076
  19.9 7.9 %collective-permute-start.1 = (bf16[8,64,128]{2,1,0:T(8,128)(2,1)S(1)}, bf16[8,64,128]{2,1,0:T(8,128)(2,1)S(1)}, u32[]{:S(2)}, u32[]{:S(2)}) collective-permute-start(bf16[8,64,128]{2,1,0:T(8,128)(2,1)S(1)} %get-tuple-element.28), channel_id=1, source_target_pairs={{1,2},{2,1},{3,4},{4,3},{5,6},{6,5},{7,8},{8,7},{9,10},{10,9},{11,... | collective-permute-start | bytes 393224 | tf_op jit(solution)/shard_map/ppermute | solution.py:423
  25.2 2.6 %collective-permute-start = (bf16[8,64,128]{2,1,0:T(8,128)(2,1)S(1)}, bf16[8,64,128]{2,1,0:T(8,128)(2,1)S(1)}, u32[]{:S(2)}, u32[]{:S(2)}) collective-permute-start(bf16[8,64,128]{2,1,0:T(8,128)(2,1)S(1)} %get-tuple-element.29), channel_id=1, source_target_pairs={{0,1},{1,0},{2,3},{3,2},{4,5},{5,4},{6,7},{7,6},{8,9},{9,8},{10,11... | collective-permute-start | bytes 393224 | tf_op jit(solution)/shard_map/ppermute | solution.py:422
  25.3 0.9 %copy-start = (f32[8,17,17]{2,0,1:T(8,128)S(1)}, f32[8,17,17]{2,0,1:T(8,128)}, u32[]{:S(2)}) copy-start(f32[8,17,17]{2,0,1:T(8,128)} %param.10) | copy-start | bytes 27748
  31.3 18.3 %all-to-all-start.1 = ((f32[32,1,640]{2,1,0:T(1,128)}), f32[32,1,640]{2,1,0:T(1,128)S(1)}, u32[]{:S(2)}, u32[]{:S(2)}) async-start(f32[32,1,640]{2,1,0:T(1,128)} %get-tuple-element.23), calls=%async_computation.1 | async-start | bytes 163840 | tf_op jit(solution)/shard_map/all_to_all | solution.py:430
  41.4 3.8 %collective-permute-start.2 = (bf16[8,64,128]{2,1,0:T(8,128)(2,1)S(1)}, bf16[8,64,128]{2,1,0:T(8,128)(2,1)S(1)}, u32[]{:S(2)}, u32[]{:S(2)}) collective-permute-start(bf16[8,64,128]{2,1,0:T(8,128)(2,1)S(1)} %get-tuple-element.21), channel_id=1, source_target_pairs={{0,1},{1,0},{2,3},{3,2},{4,5},{5,4},{6,7},{7,6},{8,9},{9,8},{10,11... | collective-permute-start | bytes 393224 | tf_op jit(solution)/shard_map/ppermute | solution.py:429
  41.7 6.6 %collective-permute-start.3 = (bf16[8,64,128]{2,1,0:T(8,128)(2,1)S(1)}, bf16[8,64,128]{2,1,0:T(8,128)(2,1)S(1)}, u32[]{:S(2)}, u32[]{:S(2)}) collective-permute-start(bf16[8,64,128]{2,1,0:T(8,128)(2,1)S(1)} %get-tuple-element.22), channel_id=1, source_target_pairs={{1,2},{2,1},{3,4},{4,3},{5,6},{6,5},{7,8},{8,7},{9,10},{10,9},{11,... | collective-permute-start | bytes 393224 | tf_op jit(solution)/shard_map/ppermute | solution.py:428

commit v7 on v6

--- a/solution.py
+++ b/solution.py
@@ -186,7 +186,8 @@
     x_ref,
     inner_ref,
     outer_ref,
-    dq_ref,
+    low_ref,
+    kt_ref,
     own_ref,
     out_inner_ref,
     out_outer_ref,
@@ -194,7 +195,6 @@
     sums_ref,
     skew_ref,
     kv_ref,
-    kt_ref,
     p_ref,
 ):
     col = lax.axis_index("col")
@@ -267,12 +267,7 @@
             qg_ref[256 * i : 256 * i + 256],
             preferred_element_type=jnp.float32,
         )
-        grad_query = jnp.dot(
-            kt_ref[:, 256 * first : 256 * (first + count)],
-            grad_low,
-            preferred_element_type=jnp.float32,
-        )
-        dq_ref[i] = (grad_query * 0.125).astype(jnp.bfloat16)
+        low_ref[i, 0 : 256 * count] = grad_low
         for step in steps:
             at = 256 * (step - steps[0])
             j = i - 1 + step
@@ -298,24 +293,46 @@
     return pl.pallas_call(
         main_kernel,
         out_shape=(
-            halo,
+            jax.ShapeDtypeStruct((8, 768, 128), jnp.bfloat16),
+            jax.ShapeDtypeStruct((64, 2048), jnp.bfloat16),
             jax.ShapeDtypeStruct((8, 128, 128), jnp.float32),
             halo,
             halo,
             jax.ShapeDtypeStruct((col_count, 1, 640), jnp.float32),
         ),
         in_specs=[VMEM_SPEC] * 7,
-        out_specs=(VMEM_SPEC,) * 5,
+        out_specs=(VMEM_SPEC,) * 6,
         scratch_shapes=[
             pltpu.VMEM((3, 4, 8, 8, 128), jnp.float32),
             pltpu.VMEM((17, 4, 8, 128), jnp.float32),
             pltpu.VMEM((2048, 128), jnp.bfloat16),
-            pltpu.VMEM((64, 2048), jnp.bfloat16),
             pltpu.VMEM((8, 256, 128), jnp.float32),
         ],
         compiler_params=pltpu.CompilerParams(vmem_limit_bytes=24 << 20),
         name="attention_backward",
     )(occupied, table, qg, scores, blocks, inner, outer)
+
+
+def query_kernel(low_ref, kt_ref, dq_ref):
+    for i in range(8):
+        _, first, count = window(i)
+        grad_query = jnp.dot(
+            kt_ref[:, 256 * first : 256 * (first + count)],
+            low_ref[i, 0 : 256 * count],
+            preferred_element_type=jnp.float32,
+        )
+        dq_ref[i] = (grad_query * 0.125).astype(jnp.bfloat16)
+
+
+def query_gradients(low, kt):
+    return pl.pallas_call(
+        query_kernel,
+        out_shape=jax.ShapeDtypeStruct((8, 64, 128), jnp.bfloat16),
+        in_specs=[VMEM_SPEC] * 2,
+        out_specs=VMEM_SPEC,
+        compiler_params=pltpu.CompilerParams(vmem_limit_bytes=8 << 20),
+        name="query_gradients",
+    )(low, kt)
 
 
 def combine_kernel(dq_ref, own_ref, inner_ref, outer_ref, bias_ref, out_ref):
@@ -422,9 +439,10 @@
     inner = lax.ppermute(blocks[:, 128:192], "col", within)
     outer = lax.ppermute(blocks[:, 192:256], "col", between)
     bias = jnp.transpose(rel_bias, (1, 0, 2))
-    dq, own, out_inner, out_outer, bias_part = main(
+    low, kt, own, out_inner, out_outer, bias_part = main(
         occupied, *own_scores(bias, blocks), blocks, inner, outer, col_count
     )
+    dq = query_gradients(low, kt)
     outer_share = lax.ppermute(out_outer, "col", between)
     inner_share = lax.ppermute(out_inner, "col", within)
     bias_parts = lax.all_to_all(bias_part, "col", 0, 0)

time: 63.6 us -> 63.5 us (level)
    pallas_call x1 -> x2, Pallas kernels: 3.46 us -> 3.72 us  [the longest x1 3.37 us: main(): pl.pallas_call(main_kernel, out_shape=(jax.ShapeDtypeStruct((8, 768, 128)...]
  transfers between devices with their start and end apart: 5 -> 5, of which waited for: 3 -> 3; matrix products, arithmetic and copies ran while one was open for 0% -> 0% of each run, Pallas kernels for 1% -> 2%
where the time goes in v7:
time: 63.5 us; the launch traced here: 62.7 us
  blocking collectives  29.5 us (46%)
  starting transfers between devices  19.2 us (30%)
  Pallas kernels  7.25 us (11%)
  waiting for transfers between devices  5.07 us (8%)
  local copies, waits for them, and re-layouts  0.9 us (1%)
  between operations  0.72 us (1%)
    all_to_all x1, blocking collectives, shards(): blocks = lax.all_to_all(packed, 'row', 0, 0)  18 us
    all_to_all x1, blocking collectives, shards(): lax.all_to_all(combine(dq, own, inner_share, outer_share, bias_parts), 'r...  11.6 us
    all_to_all x1, starting transfers between devices, shards(): bias_parts = lax.all_to_all(bias_part, 'col', 0, 0)  10.1 us
    ppermute x1, starting transfers between devices, shards(): outer = lax.ppermute(blocks[:, 192:256], 'col', between)  5.3 us
    ppermute x1, starting transfers between devices, shards(): outer_share = lax.ppermute(out_outer, 'col', between)  3.44 us
    pallas_call x1, Pallas kernels, main(): pl.pallas_call(main_kernel, out_shape=(jax.ShapeDtypeStruct((8, 768, 128)...  3.37 us
    ppermute x1, waiting for transfers between devices, shards(): outer_share = lax.ppermute(out_outer, 'col', between)  2.77 us
    pallas_call x1, Pallas kernels, unpack(): pl.pallas_call(unpack_kernel, out_shape=(token, token, token, jax.ShapeDt...  1.52 us
  transfers between devices with their start and end apart: 5, of which 3 were waited for; matrix products, arithmetic and copies ran while one was open for 0% of the time, Pallas kernels for 2%

profile of v7, /device:TPU:1, one launch (start us, length us, event | category | flops | bytes accessed | tf_op | source)
XLA Modules:
  0.0 62.7 jit_solution(16588648441460011931)
XLA Ops:
  0.6 0.0 copy-start.1
  0.6 1.3 %pack.1 = bf16[8,256,128]{2,1,0:T(8,128)(2,1)S(1)} custom-call(bf16[8,16,512]{2,1,0:T(8,128)(2,1)} %q_hbm.1, bf16[8,16,512]{2,1,0:T(8,128)(2,1)} %k_hbm.1, bf16[8,16,512]{2,1,0:T(8,128)(2,1)} %v_hbm.1, bf16[8,16,512]{2,1,0:T(8,128)(2,1)} %g_hbm.1), custom_call_target="tpu_custom_call" | custom-call | tf_op jit(solution)/shard_map/pack/pallas_call | solution.py:68
  1.9 18.0 %all_to_all.15.x_ref = bf16[8,256,128]{2,1,0:T(8,128)(2,1)S(1)} all-to-all(bf16[8,256,128]{2,1,0:T(8,128)(2,1)S(1)} %pack.1), channel_id=1, replica_groups=mesh['row'=8,'col'=32] {'row'}, dimensions={0} | all-to-all | bytes 1048576 | tf_op jit(solution)/shard_map/all_to_all | solution.py:438
  19.9 5.3 %collective-permute-start.1 = (bf16[8,64,128]{2,1,0:T(8,128)(2,1)S(1)}, bf16[8,64,128]{2,1,0:T(8,128)(2,1)S(1)}, u32[]{:S(2)}, u32[]{:S(2)}) collective-permute-start(bf16[8,64,128]{2,1,0:T(8,128)(2,1)S(1)} %get-tuple-element.30), channel_id=1, source_target_pairs={{1,2},{2,1},{3,4},{4,3},{5,6},{6,5},{7,8},{8,7},{9,10},{10,9},{11,... | collective-permute-start | bytes 393224 | tf_op jit(solution)/shard_map/ppermute | solution.py:440
  25.2 0.1 collective-permute-start
  25.3 0.0 copy-start
  25.3 0.9 %copy-done = f32[8,17,17]{2,0,1:T(8,128)S(1)} copy-done((f32[8,17,17]{2,0,1:T(8,128)S(1)}, f32[8,17,17]{2,0,1:T(8,128)}, u32[]{:S(2)}) %copy-start) | copy-done | bytes 9272
  26.2 0.6 own_scores.1
  26.8 1.0 %collective-permute-done.1.outer_ref = bf16[8,64,128]{2,1,0:T(8,128)(2,1)S(1)} collective-permute-done((bf16[8,64,128]{2,1,0:T(8,128)(2,1)S(1)}, bf16[8,64,128]{2,1,0:T(8,128)(2,1)S(1)}, u32[]{:S(2)}, u32[]{:S(2)}) %collective-permute-start.1) | collective-permute-done | bytes 131104 | tf_op jit(solution)/shard_map/ppermute | solution.py:440
  27.9 0.0 collective-permute-done.inner_ref
  27.9 0.0 copy-done.1
  27.9 3.4 %attention_backward.1 = (bf16[8,768,128]{2,1,0:T(8,128)(2,1)S(1)}, bf16[64,2048]{1,0:T(8,128)(2,1)S(1)}, f32[8,128,128]{2,1,0:T(8,128)S(1)}, bf16[8,64,128]{2,1,...) custom-call(s32[8,32]{1,0:T(8,128)S(1)} %copy-done.1, ...), custom_call_target="tpu_custom_call" | custom-call | tf_op jit(solution)/shard_map/attention_backward/pallas_call | solution.py:293
  31.2 10.1 %all-to-all-start.1 = ((f32[32,1,640]{2,1,0:T(1,128)}), f32[32,1,640]{2,1,0:T(1,128)S(1)}, u32[]{:S(2)}, u32[]{:S(2)}) async-start(f32[32,1,640]{2,1,0:T(1,128)} %get-tuple-element.25), calls=%async_computation.1 | async-start | bytes 163840 | tf_op jit(solution)/shard_map/all_to_all | solution.py:448
  41.3 0.3 collective-permute-start.2
  41.6 3.4 %collective-permute-start.3 = (bf16[8,64,128]{2,1,0:T(8,128)(2,1)S(1)}, bf16[8,64,128]{2,1,0:T(8,128)(2,1)S(1)}, u32[]{:S(2)}, u32[]{:S(2)}) collective-permute-start(bf16[8,64,128]{2,1,0:T(8,128)(2,1)S(1)} %get-tuple-element.24), channel_id=1, source_target_pairs={{1,2},{2,1},{3,4},{4,3},{5,6},{6,5},{7,8},{8,7},{9,10},{10,9},{11,... | collective-permute-start | bytes 393224 | tf_op jit(solution)/shard_map/ppermute | solution.py:446
  45.1 0.4 query_gradients.1.dq_ref
  45.4 0.0 collective-permute-done.2.inner_ref
  45.4 2.8 %collective-permute-done.3.outer_ref = bf16[8,64,128]{2,1,0:T(8,128)(2,1)S(1)} collective-permute-done((bf16[8,64,128]{2,1,0:T(8,128)(2,1)S(1)}, bf16[8,64,128]{2,1,0:T(8,128)(2,1)S(1)}, u32[]{:S(2)}, u32[]{:S(2)}) %collective-permute-start.3) | collective-permute-done | bytes 131104 | tf_op jit(solution)/shard_map/ppermute | solution.py:446
  48.2 1.3 %all-to-all-done.1.bias_ref = f32[32,1,640]{2,1,0:T(1,128)S(1)} async-done(((f32[32,1,640]{2,1,0:T(1,128)}), f32[32,1,640]{2,1,0:T(1,128)S(1)}, u32[]{:S(2)}, u32[]{:S(2)}) %all-to-all-start.1) | async-done | bytes 81952 | tf_op jit(solution)/shard_map/all_to_all | solution.py:448
  49.5 0.1 combine.1
  49.6 11.6 %all_to_all.16.z_ref = bf16[8,208,128]{2,1,0:T(8,128)(2,1)S(1)} all-to-all(bf16[8,208,128]{2,1,0:T(8,128)(2,1)S(1)} %combine.1), channel_id=1, replica_groups=mesh['row'=8,'col'=32] {'row'}, dimensions={0} | all-to-all | bytes 851968 | tf_op jit(solution)/shard_map/all_to_all | solution.py:449
  61.2 1.5 %unpack.1 = (bf16[8,16,512]{2,1,0:T(8,128)(2,1)}, bf16[8,16,512]{2,1,0:T(8,128)(2,1)}, bf16[8,16,512]{2,1,0:T(8,128)(2,1)}, f32[17,8,17]{2,1,0:T(8,128)}) custom-call(bf16[8,208,128]{2,1,0:T(8,128)(2,1)S(1)} %all_to_all.16.z_ref), custom_call_target="tpu_custom_call" | custom-call | tf_op jit(solution)/shard_map/unpack/pallas_call | solution.py:421
  (1 shorter events, 0.0 us)
Async XLA Ops:
  0.6 27.2 %copy-start.1 = (s32[8,32]{1,0:T(8,128)S(1)}, s32[8,32]{1,0:T(8,128)}, u32[]{:S(2)}) copy-start(s32[8,32]{1,0:T(8,128)} %occ_ref.1) | copy-start | bytes 3076
  19.9 7.9 %collective-permute-start.1 = (bf16[8,64,128]{2,1,0:T(8,128)(2,1)S(1)}, bf16[8,64,128]{2,1,0:T(8,128)(2,1)S(1)}, u32[]{:S(2)}, u32[]{:S(2)}) collective-permute-start(bf16[8,64,128]{2,1,0:T(8,128)(2,1)S(1)} %get-tuple-element.30), channel_id=1, source_target_pairs={{1,2},{2,1},{3,4},{4,3},{5,6},{6,5},{7,8},{8,7},{9,10},{10,9},{11,... | collective-permute-start | bytes 393224 | tf_op jit(solution)/shard_map/ppermute | solution.py:440
  25.2 2.6 %collective-permute-start = (bf16[8,64,128]{2,1,0:T(8,128)(2,1)S(1)}, bf16[8,64,128]{2,1,0:T(8,128)(2,1)S(1)}, u32[]{:S(2)}, u32[]{:S(2)}) collective-permute-start(bf16[8,64,128]{2,1,0:T(8,128)(2,1)S(1)} %get-tuple-element.31), channel_id=1, source_target_pairs={{0,1},{1,0},{2,3},{3,2},{4,5},{5,4},{6,7},{7,6},{8,9},{9,8},{10,11... | collective-permute-start | bytes 393224 | tf_op jit(solution)/shard_map/ppermute | solution.py:439
  25.3 0.9 %copy-start = (f32[8,17,17]{2,0,1:T(8,128)S(1)}, f32[8,17,17]{2,0,1:T(8,128)}, u32[]{:S(2)}) copy-start(f32[8,17,17]{2,0,1:T(8,128)} %param.10) | copy-start | bytes 27748
  31.2 18.2 %all-to-all-start.1 = ((f32[32,1,640]{2,1,0:T(1,128)}), f32[32,1,640]{2,1,0:T(1,128)S(1)}, u32[]{:S(2)}, u32[]{:S(2)}) async-start(f32[32,1,640]{2,1,0:T(1,128)} %get-tuple-element.25), calls=%async_computation.1 | async-start | bytes 163840 | tf_op jit(solution)/shard_map/all_to_all | solution.py:448
  41.3 4.1 %collective-permute-start.2 = (bf16[8,64,128]{2,1,0:T(8,128)(2,1)S(1)}, bf16[8,64,128]{2,1,0:T(8,128)(2,1)S(1)}, u32[]{:S(2)}, u32[]{:S(2)}) collective-permute-start(bf16[8,64,128]{2,1,0:T(8,128)(2,1)S(1)} %get-tuple-element.23), channel_id=1, source_target_pairs={{0,1},{1,0},{2,3},{3,2},{4,5},{5,4},{6,7},{7,6},{8,9},{9,8},{10,11... | collective-permute-start | bytes 393224 | tf_op jit(solution)/shard_map/ppermute | solution.py:447
  41.6 6.6 %collective-permute-start.3 = (bf16[8,64,128]{2,1,0:T(8,128)(2,1)S(1)}, bf16[8,64,128]{2,1,0:T(8,128)(2,1)S(1)}, u32[]{:S(2)}, u32[]{:S(2)}) collective-permute-start(bf16[8,64,128]{2,1,0:T(8,128)(2,1)S(1)} %get-tuple-element.24), channel_id=1, source_target_pairs={{1,2},{2,1},{3,4},{4,3},{5,6},{6,5},{7,8},{8,7},{9,10},{10,9},{11,... | collective-permute-start | bytes 393224 | tf_op jit(solution)/shard_map/ppermute | solution.py:446
